TPU v7x, 32 devices: a whole 2x2x4 slice. The times are simulated.
32 devices in a mesh: context: 16 (over z, x, core), tensor: 2 (over y).
Axes of the slice: x: 2, y: 2, z: 4, core: 2. Of those that a mesh axis runs over, the one named last changes fastest.
Arguments:
- query_in: bfloat16 [2, 2048, 4096], P(None, 'context', 'tensor'), may hold values from -6 to 6
- key_in: bfloat16 [2, 2048, 4096], P(None, 'context', 'tensor'), may hold values from -6 to 6
- value_in: bfloat16 [2, 2048, 4096], P(None, 'context', 'tensor'), may hold values from -6 to 6
- short_filter: float32 [3, 7, 256], P(None, None, 'tensor'), may hold values from -2.4 to 2.4
- long_filter: float32 [256, 2048], P(('tensor', 'context')), may hold values from 0 to 1
- out_weight: bfloat16 [4096, 4096], P('context', 'tensor'), may hold values from -0.09375 to 0.09375
- grad_out: bfloat16 [2, 2048, 4096], P(None, 'context', 'tensor'), may hold values from -6 to 6
Outputs:
- mixed_out: bfloat16 [2, 2048, 4096], P(None, 'context', 'tensor')
- grad_query: bfloat16 [2, 2048, 4096], P(None, 'context', 'tensor')
- grad_key: bfloat16 [2, 2048, 4096], P(None, 'context', 'tensor')
- grad_value: bfloat16 [2, 2048, 4096], P(None, 'context', 'tensor')
- grad_weight: float32 [4096, 4096], P('context', 'tensor')
- grad_long: float32 [256, 2048], P(('tensor', 'context'))
All inputs are finite; a program needn't handle non-finite values.
Results may differ from a plain program's by a relative error of at most 0.015.
Values may be sent and summed in bfloat16 or wider, within the bound.
A program may use at most 128 MiB of HBM per device.

v0:
```python
import math

import jax
import jax.numpy as jnp
from jax import lax
from jax.sharding import PartitionSpec as P

GROUP = 16
TAPS = 7


precise = lax.Precision.HIGH


def shifted(value, axis, steps):
    count = lax.axis_size(axis)
    first, last = (max(0, -steps), min(count, count - steps))
    return lax.ppermute(value, axis, [(source, source + steps) for source in range(first, last)])


def transform_table(points, direction):
    indices = jnp.arange(points, dtype=jnp.int32)
    phases = indices[:, None] * indices[None, :] % points
    angles = direction * 2.0 * math.pi / points * phases.astype(jnp.float32)
    return (jnp.cos(angles), jnp.sin(angles))


def twiddles(outer_len, inner_len, direction):
    row_index = jnp.arange(outer_len, dtype=jnp.int32)[:, None]
    column_index = jnp.arange(inner_len, dtype=jnp.int32)[None, :]
    phases = row_index * column_index % (outer_len * inner_len)
    angles = direction * 2.0 * math.pi / (outer_len * inner_len) * phases.astype(jnp.float32)
    return (jnp.cos(angles)[None, :, :, None], jnp.sin(angles)[None, :, :, None])


def complex_product(first_pair, second_pair):
    return (
        first_pair[0] * second_pair[0] - first_pair[1] * second_pair[1],
        first_pair[0] * second_pair[1] + first_pair[1] * second_pair[0],
    )


def conjugate(number_pair):
    return (number_pair[0], -number_pair[1])


def forward_transform(signal, outer_len, inner_len):
    batches, points, channels = signal.shape
    folded = signal.reshape(batches, outer_len, inner_len, channels)
    cos_outer, sin_outer = transform_table(outer_len, -1.0)
    partial_value = (
        jnp.einsum("kn,bnmc->bkmc", cos_outer, folded, precision=precise),
        jnp.einsum("kn,bnmc->bkmc", sin_outer, folded, precision=precise),
    )
    partial_value = complex_product(partial_value, twiddles(outer_len, inner_len, -1.0))
    cos_inner, sin_inner = transform_table(inner_len, -1.0)
    real_part = jnp.einsum(
        "bkmc,mj->bkjc", partial_value[0], cos_inner, precision=precise
    ) - jnp.einsum("bkmc,mj->bkjc", partial_value[1], sin_inner, precision=precise)
    imag_part = jnp.einsum(
        "bkmc,mj->bkjc", partial_value[0], sin_inner, precision=precise
    ) + jnp.einsum("bkmc,mj->bkjc", partial_value[1], cos_inner, precision=precise)
    return (real_part, imag_part)


def inverse_transform(spectrum, keep_rows):
    batches, outer_len, inner_len, channels = spectrum[0].shape
    cos_inner, sin_inner = transform_table(inner_len, 1.0)
    partial_value = (
        jnp.einsum("bkjc,jm->bkmc", spectrum[0], cos_inner, precision=precise)
        - jnp.einsum("bkjc,jm->bkmc", spectrum[1], sin_inner, precision=precise),
        jnp.einsum("bkjc,jm->bkmc", spectrum[0], sin_inner, precision=precise)
        + jnp.einsum("bkjc,jm->bkmc", spectrum[1], cos_inner, precision=precise),
    )
    partial_value = complex_product(partial_value, twiddles(outer_len, inner_len, 1.0))
    cos_outer, sin_outer = transform_table(outer_len, 1.0)
    real_part = jnp.einsum(
        "nk,bkmc->bnmc", cos_outer, partial_value[0], precision=precise
    ) - jnp.einsum("nk,bkmc->bnmc", sin_outer, partial_value[1], precision=precise)
    unfolded = real_part.reshape(batches, outer_len * inner_len, channels)
    return unfolded[:, :keep_rows] / float(outer_len * inner_len)


def featurize(signal, leading, tap_weights):
    local_rows = signal.shape[1]
    padded = jnp.concatenate([leading, signal], axis=1)
    summed = jnp.zeros(signal.shape, jnp.float32)
    for offset in range(TAPS):
        lead_at = TAPS - 1 - offset
        summed = summed + tap_weights[offset] * padded[:, lead_at : lead_at + local_rows].astype(
            jnp.float32
        )
    return summed


def unfeaturize(gradient, trailing, tap_weights):
    local_rows = gradient.shape[1]
    padded = jnp.concatenate([gradient, trailing], axis=1)
    summed = jnp.zeros(gradient.shape, jnp.float32)
    for offset in range(TAPS):
        summed = summed + tap_weights[offset] * padded[:, offset : offset + local_rows]
    return summed


def body(query_in, key_in, value_in, short_filter, long_filter, out_weight, grad_out):
    batches, local_rows, channels = query_in.shape
    context_size = lax.axis_size("context")
    seq_length = local_rows * context_size
    points = 2 * seq_length
    outer_len = math.gcd(points, 128)
    inner_len = points // outer_len
    grad_scale = float(batches * seq_length * GROUP) ** (-0.5)
    margin = TAPS - 1
    tap_weights = jnp.repeat(short_filter, GROUP, axis=2)
    last_rows = jnp.stack(
        [
            query_in[:, local_rows - margin :],
            key_in[:, local_rows - margin :],
            value_in[:, local_rows - margin :],
        ]
    )
    before = shifted(last_rows, "context", 1)
    query_feat = featurize(query_in, before[0], tap_weights[0])
    key_feat = featurize(key_in, before[1], tap_weights[1])
    value_feat = featurize(value_in, before[2], tap_weights[2])
    product = (key_feat * value_feat).astype(jnp.bfloat16)
    grad_full = lax.all_gather(grad_out, "tensor", axis=2, tiled=True)
    kernel = jnp.pad(long_filter, ((0, 0), (0, seq_length))).T[None]
    kernel_spec = forward_transform(kernel, outer_len, inner_len)
    kernel_spec = (
        jnp.repeat(kernel_spec[0], GROUP, axis=3),
        jnp.repeat(kernel_spec[1], GROUP, axis=3),
    )

    def padded_spectrum(blocked):
        extended = jnp.pad(blocked.astype(jnp.float32), ((0, 0), (0, seq_length), (0, 0)))
        return forward_transform(extended, outer_len, inner_len)

    product_full = lax.all_to_all(product, "context", split_axis=2, concat_axis=1, tiled=True)
    product_spec = padded_spectrum(product_full)
    conv_out = lax.all_to_all(
        inverse_transform(complex_product(product_spec, kernel_spec), seq_length).astype(
            jnp.bfloat16
        ),
        "context",
        split_axis=1,
        concat_axis=2,
        tiled=True,
    )
    gated = (query_feat * conv_out.astype(jnp.float32)).astype(jnp.bfloat16)
    weight_rows = lax.all_gather(out_weight, "context", axis=0, tiled=True)
    block_out = jnp.einsum("blc,oc->blo", gated, weight_rows, preferred_element_type=jnp.float32)
    columns = grad_full
    grad_acc = jnp.einsum("blo,oc->blc", columns, weight_rows, preferred_element_type=jnp.float32)
    grad_conv = (grad_acc * query_feat).astype(jnp.bfloat16)
    grad_conv_full = lax.all_to_all(grad_conv, "context", split_axis=2, concat_axis=1, tiled=True)
    grad_spec = padded_spectrum(grad_conv_full)
    grad_product_chan = inverse_transform(
        complex_product(grad_spec, conjugate(kernel_spec)), seq_length
    ).astype(jnp.bfloat16)
    crossed = complex_product(grad_spec, conjugate(product_spec))
    groups = crossed[0].shape[3] // GROUP
    merged = tuple(
        (
            jnp.sum(
                component.reshape(component.shape[0], outer_len, inner_len, groups, GROUP),
                axis=(0, 4),
            )[None]
            for component in crossed
        )
    )
    grad_long = inverse_transform(merged, seq_length)[0].T * grad_scale
    grad_product_chan, grad_long = (grad_product_chan, grad_long)
    grad_product = lax.all_to_all(
        grad_product_chan, "context", split_axis=1, concat_axis=2, tiled=True
    )
    mixed_out = lax.psum_scatter(
        block_out.astype(jnp.bfloat16), "tensor", scatter_dimension=2, tiled=True
    )
    columns = grad_full
    grad_weight = lax.psum_scatter(
        jnp.einsum("blo,blc->oc", columns, gated, preferred_element_type=jnp.float32).astype(
            jnp.bfloat16
        ),
        "context",
        scatter_dimension=0,
        tiled=True,
    ).astype(jnp.float32)
    product_grad = grad_product.astype(jnp.float32)
    grad_qfeat = grad_acc * conv_out.astype(jnp.float32)
    grad_kfeat = product_grad * value_feat
    grad_vfeat = product_grad * key_feat
    first_rows = jnp.stack([grad_qfeat[:, :margin], grad_kfeat[:, :margin], grad_vfeat[:, :margin]])
    following = shifted(first_rows.astype(jnp.bfloat16), "context", -1).astype(first_rows.dtype)
    grad_query = unfeaturize(grad_qfeat, following[0], tap_weights[0]).astype(jnp.bfloat16)
    grad_key = unfeaturize(grad_kfeat, following[1], tap_weights[1]).astype(jnp.bfloat16)
    grad_value = unfeaturize(grad_vfeat, following[2], tap_weights[2]).astype(jnp.bfloat16)
    return (mixed_out, grad_query, grad_key, grad_value, grad_weight, grad_long)


def solution(mesh):
    in_specs = (
        P(None, "context", "tensor"),
        P(None, "context", "tensor"),
        P(None, "context", "tensor"),
        P(None, None, "tensor"),
        P(("tensor", "context"), None),
        P("context", "tensor"),
        P(None, "context", "tensor"),
    )
    out_specs = (
        P(None, "context", "tensor"),
        P(None, "context", "tensor"),
        P(None, "context", "tensor"),
        P(None, "context", "tensor"),
        P("context", "tensor"),
        P(("tensor", "context"), None),
    )
    return jax.shard_map(body, mesh=mesh, in_specs=in_specs, out_specs=out_specs, check_vma=False)
```

profile of v0, /device:TPU:0, one launch (start us, length us, event | category | flops | bytes accessed | tf_op | source)
XLA Modules:
  0.0 734.9 jit_solution(7365557278059666580)
XLA Ops:
  14.6 30.8 %all-gather.5.cloned.1.call-done = bf16[2,128,4096]{2,1,0:T(8,128)(2,1)} async-done(((bf16[2,128,2048]{2,1,0:T(8,128)(2,1)}), bf16[2,128,4096]{2,1,0:T(8,128)(2,1)}) %all-gather.5.cloned.1.call-update) | async-done | bytes 2097168 | tf_op jit(solution)/shard_map/all_gather | solution.py:127
  45.4 128.6 %all-gather.3.cloned.1.call-done = bf16[4096,2048]{1,0:T(8,128)(2,1)} async-done(((bf16[256,2048]{1,0:T(8,128)(2,1)}), bf16[4096,2048]{1,0:T(8,128)(2,1)}) %all-gather.3.cloned.1.call-update) | async-done | bytes 16777232 | tf_op jit(solution)/shard_map/all_gather | solution.py:151
  174.0 11.5 %multiply_convert_fusion = (bf16[2,128,2048]{2,1,0:T(8,128)(2,1)S(1)}, f32[2,128,2048]{2,1,0:T(8,128)}, f32[2,128,2048]{2,1,0:T(8,128)}) fusion(bf16[2,128,2048]{2,1,0:T(8,128)(2,1)S(1)} %copy-done.70, bf16[2,6,2048]{2,1,0:T(8,128)(2,1)S(1)} %get-tuple-element.55, f32[2048]{0:T(1024)S(1)} %broadcast_in_dim.158, f32[2048]{0:T(1024)S(1)} %broadcast_in_dim.156, ...), kind=kOutput, calls=%fused_computation.179 | convolution fusion | flops 4315938816 | bytes 25272320 | tf_op jit(solution)/shard_map/blo,oc->blc/dot_general | solution.py:154
  201.9 12.5 %all-to-all-done.2 = bf16[2,128,2048]{1,0,2:T(2,128)(2,1)S(1)} async-done(((bf16[2,128,2048]{1,0,2:T(2,128)(2,1)}), bf16[2,128,2048]{1,0,2:T(2,128)(2,1)S(1)}, u32[]{:S(2)}, u32[]{:S(2)}) %all-to-all-start.2) | async-done | bytes 1048608 | tf_op jit(solution)/shard_map/all_to_all | solution.py:156
  226.3 5.2 fusion.17
  231.5 5.9 copy.151
  237.4 6.3 fusion.203
  247.8 5.5 copy.152
  253.4 6.0 convolution_add_fusion.1
  273.6 8.1 %fusion.8 = (f32[2,128,32,128]{3,2,1,0:T(8,128)S(1)}, f32[2,128,32,128]{3,2,1,0:T(8,128)}) fusion(f32[32,2,128,128]{3,0,2,1:T(8,128)} %convolution_subtract_fusion, f32[128,32]{1,0:T(8,128)S(1)} %copy.139, f32[128,32]{1,0:T(8,128)S(1)} %copy.138, f32[32,2,128,128]{3,0,2,1:T(8,128)} %fusion.191, f32[32,2,128,128]{3,0,2,1:T(8,128)S(1)} %convolution_add_fusion.1, ...), kind=kOutput, calls=%fused_computation.24 | convolution fusion | flops 211826688 | bytes 29392896 | tf_op jit(solution)/shard_map/bkjc,jm->bkmc/dot_general | solution.py:73
  281.7 6.3 fusion.24
  295.0 9.7 %copy.159 = bf16[2,2048,128]{2,0,1:T(2,128)(2,1)} copy(bf16[2,2048,128]{2,1,0:T(8,128)(2,1)S(1)} %fusion.91) | data formatting | bytes 2097152 | tf_op jit(solution)/shard_map/convert_element_type | solution.py:160
  304.7 6.7 all-to-all-start.3
  324.5 9.9 %all-to-all-done.3 = bf16[2,2048,128]{2,0,1:T(2,128)(2,1)S(1)} async-done(((bf16[2,2048,128]{2,0,1:T(2,128)(2,1)}), bf16[2,2048,128]{2,0,1:T(2,128)(2,1)S(1)}, u32[]{:S(2)}, u32[]{:S(2)}) %all-to-all-start.3) | async-done | bytes 1048608 | tf_op jit(solution)/shard_map/all_to_all | solution.py:174
  344.3 6.8 all-to-all-start
  356.1 17.9 %all-to-all-done = bf16[2,128,2048]{1,0,2:T(2,128)(2,1)S(1)} async-done(((bf16[2,128,2048]{1,0,2:T(2,128)(2,1)}), bf16[2,128,2048]{1,0,2:T(2,128)(2,1)S(1)}, u32[]{:S(2)}, u32[]{:S(2)}) %all-to-all-start) | async-done | bytes 1048608 | tf_op jit(solution)/shard_map/all_to_all | solution.py:139
  386.0 5.2 fusion.23
  391.1 5.5 copy.128
  396.6 6.2 fusion.206
  406.9 5.6 copy.129
  412.6 6.0 convolution_add_fusion.3
  418.6 11.8 %fusion.15 = (f32[128,32,128]{2,1,0:T(8,128)}, f32[128,32,128]{2,1,0:T(8,128)}, f32[32,2,128,128]{3,0,2,1:T(8,128)}) fusion(f32[32,2,128,128]{3,0,2,1:T(8,128)S(1)} %copy-done.1, f32[32,2,128,128]{3,0,2,1:T(8,128)S(1)} %copy-done.3, f32[32,2,128,128]{3,0,2,1:T(8,128)S(1)} %convolution_add_fusion.3, f32[32,2,128,128]{3,0,2,1:T(8,128)} %fusion.201, ...), kind=kOutput, calls=%fused_computation.37 | convolution fusion | flops 210778112 | bytes 29360128 | tf_op jit(solution)/shard_map/bkmc,mj->bkjc/dot_general | solution.py:59
  439.6 4.9 convolution_subtract_fusion.2
  444.5 7.9 %fusion.18 = (f32[2,128,32,128]{3,2,1,0:T(8,128)S(1)}, f32[2,128,32,128]{3,2,1,0:T(8,128)}) fusion(f32[32,2,128,128]{3,0,2,1:T(8,128)} %convolution_subtract_fusion.2, f32[128,32]{1,0:T(8,128)S(1)} %copy.139, f32[128,32]{1,0:T(8,128)S(1)} %copy.138, f32[32,2,128,128]{3,0,2,1:T(8,128)} %fusion.194, f32[32,2,128,128]{3,0,2,1:T(8,128)S(1)} %convolution_add_fusion.3, ...), kind=kOutput, calls=%fused_computation.50 | convolution fusion | flops 211826688 | bytes 29392896 | tf_op jit(solution)/shard_map/bkjc,jm->bkmc/dot_general | solution.py:73
  452.4 6.3 fusion.28
  465.7 9.1 %copy.143 = bf16[2,2048,128]{2,0,1:T(2,128)(2,1)S(1)} copy(bf16[2,2048,128]{2,1,0:T(8,128)(2,1)S(1)} %fusion.92) | data formatting | bytes 2097152 | tf_op jit(solution)/shard_map/convert_element_type | solution.py:142
  474.8 31.5 %all_to_all.16 = bf16[2,2048,128]{2,0,1:T(2,128)(2,1)S(1)} all-to-all(bf16[2,2048,128]{2,0,1:T(2,128)(2,1)S(1)} %copy.143), channel_id=1, replica_groups=mesh['context'=16,'tensor'=2] {'context'}, dimensions={1} | all-to-all | bytes 2097152 | tf_op jit(solution)/shard_map/all_to_all | solution.py:141
  508.4 8.2 %fusion.4 = bf16[4096,2048]{0,1:T(8,128)(2,1)} fusion(bf16[2,128,2048]{2,1,0:T(8,128)(2,1)S(1)} %get-tuple-element.47, bf16[2,128,4096]{2,1,0:T(8,128)(2,1)S(1)} %copy-done.18), kind=kOutput, calls=%fused_computation.5 | convolution fusion | flops 4303355904 | bytes 19922944 | tf_op jit(solution)/shard_map/blo,blc->oc/dot_general | solution.py:182
  530.2 21.0 %fusion.5 = bf16[2,128,4096]{2,1,0:T(8,128)(2,1)} fusion(bf16[2,128,2048]{2,1,0:T(8,128)(2,1)S(1)} %get-tuple-element.47, bf16[4096,2048]{1,0:T(8,128)(2,1)} %all-gather.3.cloned.1.call-done), kind=kOutput, calls=%fused_computation.21 | convolution fusion | flops 4296015872 | bytes 19922944 | tf_op jit(solution)/shard_map/blc,oc->blo/dot_general | solution.py:152
  559.3 8.3 %fusion.74 = bf16[2,128,2048]{2,1,0:T(8,128)(2,1)} fusion(f32[2,6,2048]{2,1,0:T(8,128)S(1)} %get-tuple-element.50, f32[2,128,2048]{2,1,0:T(8,128)} %get-tuple-element.46, f32[2048]{0:T(1024)S(1)} %copy-done.56, f32[2048]{0:T(1024)S(1)} %copy-done.58, f32[2048]{0:T(1024)S(1)} %copy-done.60, f32[2048]{0:T(1024)S(1)} %copy-done.62, f32[2048]{0:T(1024)S(1)} %copy-done.64, ...), kind=kLoop, calls=%fused_computation.138 | loop fusion | flops 10485760 | bytes 3301376 | tf_op jit(solution)/shard_map/convert_element_type | solution.py:195
  573.8 120.6 %reduce-scatter.5.cloned.1.call-done = bf16[256,2048]{0,1:T(8,128)(2,1)} async-done(((bf16[4096,2048]{0,1:T(8,128)(2,1)}), bf16[256,2048]{0,1:T(8,128)(2,1)}) %reduce-scatter.5.cloned.1.call-update) | async-done | bytes 1048592 | tf_op jit(solution)/shard_map/reduce_scatter | solution.py:181
  697.0 31.2 %reduce-scatter.3.cloned.1.call-done = bf16[2,128,2048]{2,1,0:T(8,128)(2,1)} async-done(((bf16[2,128,4096]{2,1,0:T(8,128)(2,1)}), bf16[2,128,2048]{2,1,0:T(8,128)(2,1)}) %reduce-scatter.3.cloned.1.call-update) | async-done | bytes 1048592 | tf_op jit(solution)/shard_map/reduce_scatter | solution.py:177
  (277 shorter events, 152.7 us)
Async XLA Ops:
  7.2 38.2 %all-gather.5.cloned.1.call-start = ((), (), s32[]{:S(2)}) async-start(), calls=%async_computation.8 | async-start | bytes 3145728 | tf_op jit(solution)/shard_map/all_gather | solution.py:127
  7.9 166.1 %all-gather.3.cloned.1.call-start = ((), (), s32[]{:S(2)}) async-start(), calls=%async_computation.6 | async-start | bytes 17825792 | tf_op jit(solution)/shard_map/all_gather | solution.py:151
  9.7 4.2 collective-permute-start
  12.9 172.7 %copy-start.55 = (f32[2048]{0:T(1024)}, f32[2048]{0:T(1024)S(1)}, u32[]{:S(2)}) copy-start(f32[2048]{0:T(1024)S(1)} %broadcast_in_dim.158) | copy-start | bytes 24580
  13.0 172.5 %copy-start.57 = (f32[2048]{0:T(1024)}, f32[2048]{0:T(1024)S(1)}, u32[]{:S(2)}) copy-start(f32[2048]{0:T(1024)S(1)} %broadcast_in_dim.156) | copy-start | bytes 24580
  13.2 172.3 %copy-start.59 = (f32[2048]{0:T(1024)}, f32[2048]{0:T(1024)S(1)}, u32[]{:S(2)}) copy-start(f32[2048]{0:T(1024)S(1)} %broadcast_in_dim.154) | copy-start | bytes 24580
  13.4 172.2 %copy-start.61 = (f32[2048]{0:T(1024)}, f32[2048]{0:T(1024)S(1)}, u32[]{:S(2)}) copy-start(f32[2048]{0:T(1024)S(1)} %broadcast_in_dim.152) | copy-start | bytes 24580
  13.6 172.0 %copy-start.63 = (f32[2048]{0:T(1024)}, f32[2048]{0:T(1024)S(1)}, u32[]{:S(2)}) copy-start(f32[2048]{0:T(1024)S(1)} %broadcast_in_dim.150) | copy-start | bytes 24580
  13.7 171.9 %copy-start.65 = (f32[2048]{0:T(1024)}, f32[2048]{0:T(1024)S(1)}, u32[]{:S(2)}) copy-start(f32[2048]{0:T(1024)S(1)} %broadcast_in_dim.148) | copy-start | bytes 24580
  13.9 171.7 %copy-start.67 = (f32[2048]{0:T(1024)}, f32[2048]{0:T(1024)S(1)}, u32[]{:S(2)}) copy-start(f32[2048]{0:T(1024)S(1)} %broadcast_in_dim.146) | copy-start | bytes 24580
  187.6 26.7 %all-to-all-start.2 = ((bf16[2,128,2048]{1,0,2:T(2,128)(2,1)}), bf16[2,128,2048]{1,0,2:T(2,128)(2,1)S(1)}, u32[]{:S(2)}, u32[]{:S(2)}) async-start(bf16[2,128,2048]{1,0,2:T(2,128)(2,1)} %copy.146), calls=%async_computation.3 | async-start | bytes 2097152 | tf_op jit(solution)/shard_map/all_to_all | solution.py:156
  201.2 15.9 %copy-start.28 = (f32[128,32]{0,1:T(8,128)}, f32[128,32]{0,1:T(8,128)S(1)}, u32[]{:S(2)}) copy-start(f32[128,32]{0,1:T(8,128)S(1)} %get-tuple-element.84) | copy-start | bytes 49156
  259.4 14.2 %copy-start = (f32[32,2,128,128]{3,0,2,1:T(8,128)}, f32[32,2,128,128]{3,0,2,1:T(8,128)S(1)}, u32[]{:S(2)}) copy-start(f32[32,2,128,128]{3,0,2,1:T(8,128)S(1)} %convolution_add_fusion.1) | copy-start | bytes 12582916
  262.5 11.1 %copy-start.2 = (f32[32,2,128,128]{3,0,2,1:T(8,128)}, f32[32,2,128,128]{3,0,2,1:T(8,128)S(1)}, u32[]{:S(2)}) copy-start(f32[32,2,128,128]{3,0,2,1:T(8,128)S(1)} %convolution_subtract_fusion.1) | copy-start | bytes 12582916
  304.7 29.6 %all-to-all-start.3 = ((bf16[2,2048,128]{2,0,1:T(2,128)(2,1)}), bf16[2,2048,128]{2,0,1:T(2,128)(2,1)S(1)}, u32[]{:S(2)}, u32[]{:S(2)}) async-start(bf16[2,2048,128]{2,0,1:T(2,128)(2,1)} %copy.159), calls=%async_computation.4 | async-start | bytes 2097152 | tf_op jit(solution)/shard_map/all_to_all | solution.py:174
  311.4 23.0 %copy-start.23 = (bf16[2,6,2048]{2,1,0:T(8,128)(2,1)S(1)}, bf16[2,6,2048]{2,1,0:T(8,128)(2,1)}, u32[]{:S(2)}) copy-start(bf16[2,6,2048]{2,1,0:T(8,128)(2,1)} %get-tuple-element.54) | copy-start | bytes 147460
  311.9 26.8 %copy-start.30 = (f32[2048]{0:T(1024)}, f32[2048]{0:T(1024)S(1)}, u32[]{:S(2)}) copy-start(f32[2048]{0:T(1024)S(1)} %broadcast_in_dim.168) | copy-start | bytes 24580
  312.1 26.6 %copy-start.32 = (f32[2048]{0:T(1024)}, f32[2048]{0:T(1024)S(1)}, u32[]{:S(2)}) copy-start(f32[2048]{0:T(1024)S(1)} %broadcast_in_dim.166) | copy-start | bytes 24580
  312.3 26.4 %copy-start.34 = (f32[2048]{0:T(1024)}, f32[2048]{0:T(1024)S(1)}, u32[]{:S(2)}) copy-start(f32[2048]{0:T(1024)S(1)} %broadcast_in_dim.164) | copy-start | bytes 24580
  312.5 26.3 %copy-start.36 = (f32[2048]{0:T(1024)}, f32[2048]{0:T(1024)S(1)}, u32[]{:S(2)}) copy-start(f32[2048]{0:T(1024)S(1)} %broadcast_in_dim.162) | copy-start | bytes 24580
  324.5 10.0 %copy-start.38 = (f32[2048]{0:T(1024)S(1)}, f32[2048]{0:T(1024)}, u32[]{:S(2)}) copy-start(f32[2048]{0:T(1024)} %broadcast_in_dim.160) | copy-start | bytes 24580
  342.3 8.9 %copy-start.22 = (f32[128,32,8]{0,2,1:T(8,128)S(1)}, f32[128,32,8]{0,2,1:T(8,128)}, u32[]{:S(2)}) copy-start(f32[128,32,8]{0,2,1:T(8,128)} %copy-done.21) | copy-start | bytes 393220
  344.3 29.7 %all-to-all-start = ((bf16[2,128,2048]{1,0,2:T(2,128)(2,1)}), bf16[2,128,2048]{1,0,2:T(2,128)(2,1)S(1)}, u32[]{:S(2)}, u32[]{:S(2)}) async-start(bf16[2,128,2048]{1,0,2:T(2,128)(2,1)} %copy.123), calls=%async_computation | async-start | bytes 2097152 | tf_op jit(solution)/shard_map/all_to_all | solution.py:139
  351.1 343.3 %reduce-scatter.5.cloned.1.call-start = ((), (), s32[]{:S(2)}) async-start(), calls=%async_computation.9 | async-start | bytes 17825792 | tf_op jit(solution)/shard_map/reduce_scatter | solution.py:181
  418.6 11.8 %copy-start.6 = (f32[128,32,128]{2,1,0:T(8,128)S(1)}, f32[128,32,128]{2,1,0:T(8,128)}, u32[]{:S(2)}) copy-start(f32[128,32,128]{2,1,0:T(8,128)} %copy.137) | copy-start | bytes 6291460
  474.8 31.7 %copy-start.16 = (f32[2,128,2048]{2,1,0:T(8,128)S(1)}, f32[2,128,2048]{2,1,0:T(8,128)}, u32[]{:S(2)}) copy-start(f32[2,128,2048]{2,1,0:T(8,128)} %get-tuple-element.37) | copy-start | bytes 6291460
  474.8 31.7 %copy-start.17 = (f32[2,128,2048]{2,1,0:T(8,128)S(1)}, f32[2,128,2048]{2,1,0:T(8,128)}, u32[]{:S(2)}) copy-start(f32[2,128,2048]{2,1,0:T(8,128)} %get-tuple-element.77) | copy-start | bytes 6291460
  516.6 211.5 %reduce-scatter.3.cloned.1.call-start = ((), (), s32[]{:S(2)}) async-start(), calls=%async_computation.7 | async-start | bytes 3145728 | tf_op jit(solution)/shard_map/reduce_scatter | solution.py:177
  554.8 4.3 collective-permute-start.1
  559.2 8.5 %copy-start.14 = (f32[2,128,2048]{2,1,0:T(8,128)S(1)}, f32[2,128,2048]{2,1,0:T(8,128)}, u32[]{:S(2)}) copy-start(f32[2,128,2048]{2,1,0:T(8,128)} %get-tuple-element.32) | copy-start | bytes 6291460
  559.2 8.5 %copy-start.31 = (f32[2048]{0:T(1024)S(1)}, f32[2048]{0:T(1024)}, u32[]{:S(2)}) copy-start(f32[2048]{0:T(1024)} %copy-done.30) | copy-start | bytes 24580
  559.2 8.5 %copy-start.33 = (f32[2048]{0:T(1024)S(1)}, f32[2048]{0:T(1024)}, u32[]{:S(2)}) copy-start(f32[2048]{0:T(1024)} %copy-done.32) | copy-start | bytes 24580
  (48 other events, 203.3 us)
Sparse Core Ops, SparseCore 0:
  9.5 35.8 all-gather.4
  47.6 126.4 all-gather.2
  516.8 177.6 reduce-scatter.4
  697.1 30.9 reduce-scatter.2
where the time goes:
time: 746 us; the launch traced here: 735 us
  waiting for transfers between devices  355 us (48%)
  matrix products  172 us (23%)
  local copies, waits for them, and re-layouts  113 us (15%)
  blocking collectives  31.5 us (4%)
  other arithmetic  26.9 us (4%)
  starting transfers between devices  21.2 us (3%)
  between operations  15.2 us (2%)
    all_gather x1, waiting for transfers between devices, body(): weight_rows = lax.all_gather(out_weight, 'context', axis=0, tiled=True)  129 us
    reduce_scatter x1, waiting for transfers between devices, body(): lax.psum_scatter(jnp.einsum('blo,blc->oc', columns, gated, preferred_elem...  121 us
    all_to_all x1, blocking collectives, body(): lax.all_to_all(inverse_transform(complex_product(product_spec, kernel_spe...  31.5 us
    reduce_scatter x1, waiting for transfers between devices, body(): lax.psum_scatter(block_out.astype(jnp.bfloat16), 'tensor', scatter_dimens...  31.2 us
    all_gather x1, waiting for transfers between devices, body(): grad_full = lax.all_gather(grad_out, 'tensor', axis=2, tiled=True)  30.8 us
    dot_general x1, matrix products, body(): jnp.einsum('blc,oc->blo', gated, weight_rows, preferred_element_type=jnp....  21 us
    all_to_all x1, waiting for transfers between devices, body(): lax.all_to_all(product, 'context', split_axis=2, concat_axis=1, tiled=True)  17.9 us
    dot_general x3, matrix products, inverse_transform(): jnp.einsum('bkjc,jm->bkmc', spectrum[1], cos_inner, precision=precise)  16.3 us
  transfers between devices with their start and end apart: 9, of which 8 were waited for; matrix products, arithmetic and copies ran while one was open for 11% of the time, Pallas kernels for 0%

commit v1 on v0

v1 whole, which is shorter than its diff:
```python
import functools

import jax
import jax.numpy as jnp
from jax import lax
from jax.experimental import pallas as pl
from jax.experimental.pallas import tpu as pltpu
from jax.sharding import PartitionSpec as P

GROUP = 16
TAPS = 7
BLOCK = 256
HALF = 128
VMEM_LIMIT = 60 * 1024 * 1024


def shifted(value, axis, steps):
    count = lax.axis_size(axis)
    first, last = (max(0, -steps), min(count, count - steps))
    return lax.ppermute(value, axis, [(source, source + steps) for source in range(first, last)])


def whole_vmem(count):
    return [pl.BlockSpec(memory_space=pltpu.VMEM)] * count


def band_kernel(filter_ref, band_ref):
    groups, length = filter_ref.shape
    zeros = jnp.zeros((HALF, HALF), jnp.float32)

    def one_group(g, carry):
        row = jnp.broadcast_to(filter_ref[pl.ds(g, 1), :], (HALF, length))
        padded = jnp.concatenate([row, zeros], axis=1)
        rolled = pltpu.roll(padded, 0, 1, stride=1, stride_axis=0).astype(jnp.bfloat16)
        band_ref[g, 0:HALF, :] = rolled[:, :length]
        band_ref[g, HALF:BLOCK, :] = jnp.concatenate(
            [jnp.zeros((HALF, HALF), jnp.bfloat16), rolled[:, : length - HALF]], axis=1
        )
        return carry

    lax.fori_loop(0, groups, one_group, 0)


def make_band(long_filter):
    groups, length = long_filter.shape
    return pl.pallas_call(
        band_kernel,
        out_shape=jax.ShapeDtypeStruct((groups, BLOCK, length), jnp.bfloat16),
        in_specs=whole_vmem(1),
        out_specs=pl.BlockSpec(memory_space=pltpu.VMEM),
        compiler_params=pltpu.CompilerParams(vmem_limit_bytes=VMEM_LIMIT),
        cost_estimate=pl.CostEstimate(
            flops=0, bytes_accessed=groups * BLOCK * length * 2, transcendentals=0
        ),
        name="band",
    )(long_filter)


def exchange_matrix():
    row = lax.broadcasted_iota(jnp.int32, (BLOCK, BLOCK), 0)
    column = lax.broadcasted_iota(jnp.int32, (BLOCK, BLOCK), 1)
    return jnp.where(row + column == BLOCK - 1, 1.0, 0.0).astype(jnp.bfloat16)


def group_mask(g, rows, columns, channels):
    lane = lax.broadcasted_iota(jnp.int32, (rows, columns), 1)
    return (lane % channels) // GROUP == g


def correlate(band_ref, work_ref, total_ref, groups, channels):
    length, columns = work_ref.shape
    blocks = length // BLOCK
    total_ref[...] = jnp.zeros_like(total_ref)

    def one_group(g, carry):
        mask = group_mask(g, 1, columns, channels).astype(jnp.bfloat16)
        masked = work_ref[...] * mask
        for j in range(blocks):
            rows = slice(j * BLOCK, (j + 1) * BLOCK)
            total_ref[rows, :] += jnp.dot(
                band_ref[g, :, : (blocks - j) * BLOCK],
                masked[j * BLOCK :, :],
                preferred_element_type=jnp.float32,
            )
        return carry

    lax.fori_loop(0, groups, one_group, 0)


def load_block(source_ref, j):
    batches, local_rows, channels = source_ref.shape[1:]
    first, count = j * BLOCK // local_rows, BLOCK // local_rows
    return jnp.concatenate(
        [
            source_ref[first : first + count, b].reshape(BLOCK, channels)
            for b in range(batches)
        ],
        axis=1,
    )


def store_block(target_ref, j, value):
    batches, local_rows, channels = target_ref.shape[1:]
    first, count = j * BLOCK // local_rows, BLOCK // local_rows
    for b in range(batches):
        target_ref[first : first + count, b] = value[
            :, b * channels : (b + 1) * channels
        ].reshape(count, local_rows, channels)


def forward_kernel(band_ref, product_ref, out_ref, work_ref, total_ref):
    groups = band_ref.shape[0]
    length, channels = work_ref.shape[0], product_ref.shape[3]
    blocks = length // BLOCK
    exchange = exchange_matrix()
    for j in range(blocks):
        block = load_block(product_ref, j)
        mirror = slice((blocks - 1 - j) * BLOCK, (blocks - j) * BLOCK)
        work_ref[mirror, :] = jnp.dot(
            exchange, block, preferred_element_type=jnp.float32
        ).astype(jnp.bfloat16)
    correlate(band_ref, work_ref, total_ref, groups, channels)
    for j in range(blocks):
        mirror = slice((blocks - 1 - j) * BLOCK, (blocks - j) * BLOCK)
        rounded = total_ref[mirror, :].astype(jnp.bfloat16)
        value = jnp.dot(exchange, rounded, preferred_element_type=jnp.float32)
        store_block(out_ref, j, value.astype(jnp.bfloat16))


def backward_kernel(band_ref, grad_ref, out_ref, work_ref, total_ref):
    groups = band_ref.shape[0]
    length, channels = work_ref.shape[0], grad_ref.shape[3]
    blocks = length // BLOCK
    for j in range(blocks):
        rows = slice(j * BLOCK, (j + 1) * BLOCK)
        work_ref[rows, :] = load_block(grad_ref, j)
    correlate(band_ref, work_ref, total_ref, groups, channels)
    for j in range(blocks):
        rows = slice(j * BLOCK, (j + 1) * BLOCK)
        store_block(out_ref, j, total_ref[rows, :].astype(jnp.bfloat16))


def long_grad_kernel(scale, grad_ref, product_ref, out_ref, grad_work, product_work, sums):
    groups, length = out_ref.shape
    channels = grad_ref.shape[3]
    blocks = length // BLOCK
    wide = grad_work.shape[1] // blocks
    exchange = exchange_matrix()
    for j in range(blocks):
        columns = slice(j * wide, (j + 1) * wide)
        grad_work[:, columns] = load_block(grad_ref, j)
        product_work[:, columns] = jnp.dot(
            exchange, load_block(product_ref, j), preferred_element_type=jnp.float32
        ).astype(jnp.bfloat16)
    sums[:, length:] = jnp.zeros_like(sums[:, length:])

    def one_group(g, carry):
        mask = group_mask(g, 1, blocks * wide, channels).astype(jnp.bfloat16)
        masked = product_work[...] * mask
        for d in range(blocks):
            sums[:, d * BLOCK : (d + 1) * BLOCK] = lax.dot_general(
                grad_work[:, d * wide :],
                masked[:, : (blocks - d) * wide],
                (((1,), (1,)), ((), ())),
                preferred_element_type=jnp.float32,
            )
        low = sums[0:HALF, :]
        high = sums[HALF:BLOCK, :]
        folded = low + jnp.concatenate(
            [jnp.zeros((HALF, HALF), jnp.float32), high[:, : length + BLOCK - HALF]], axis=1
        )
        rolled = pltpu.roll(folded, 0, 1, stride=1, stride_axis=0)
        summed = jnp.sum(rolled, axis=0, keepdims=True)
        placed = pltpu.roll(
            jnp.broadcast_to(summed, (8, length + BLOCK)), length + 1, 1
        )
        out_ref[pl.ds(g, 1), :] = placed[0:1, :length] * scale
        return carry

    lax.fori_loop(0, groups, one_group, 0)


def correlation_call(kernel, name, band, signal):
    owners, batches, local_rows, channels = signal.shape
    length = owners * local_rows
    groups = band.shape[0]
    columns = batches * channels
    return pl.pallas_call(
        kernel,
        out_shape=jax.ShapeDtypeStruct(signal.shape, jnp.bfloat16),
        in_specs=whole_vmem(2),
        out_specs=pl.BlockSpec(memory_space=pltpu.VMEM),
        scratch_shapes=[
            pltpu.VMEM((length, columns), jnp.bfloat16),
            pltpu.VMEM((length, columns), jnp.float32),
        ],
        compiler_params=pltpu.CompilerParams(vmem_limit_bytes=VMEM_LIMIT),
        cost_estimate=pl.CostEstimate(
            flops=groups * length * length * columns,
            bytes_accessed=band.size * 2 + signal.size * 4,
            transcendentals=0,
        ),
        name=name,
    )(band, signal)


def long_grad_call(grad, product, groups, scale):
    owners, batches, local_rows, channels = grad.shape
    length = owners * local_rows
    blocks = length // BLOCK
    columns = batches * channels
    return pl.pallas_call(
        functools.partial(long_grad_kernel, scale),
        out_shape=jax.ShapeDtypeStruct((groups, length), jnp.float32),
        in_specs=whole_vmem(2),
        out_specs=pl.BlockSpec(memory_space=pltpu.VMEM),
        scratch_shapes=[
            pltpu.VMEM((BLOCK, blocks * columns), jnp.bfloat16),
            pltpu.VMEM((BLOCK, blocks * columns), jnp.bfloat16),
            pltpu.VMEM((BLOCK, length + BLOCK), jnp.float32),
        ],
        compiler_params=pltpu.CompilerParams(vmem_limit_bytes=VMEM_LIMIT),
        cost_estimate=pl.CostEstimate(
            flops=groups * length * length * columns,
            bytes_accessed=grad.size * 4 + groups * length * 4,
            transcendentals=0,
        ),
        name="long_grad",
    )(grad, product)


def featurize(signal, leading, tap_weights):
    local_rows = signal.shape[1]
    padded = jnp.concatenate([leading, signal], axis=1)
    summed = jnp.zeros(signal.shape, jnp.float32)
    for offset in range(TAPS):
        lead_at = TAPS - 1 - offset
        summed = summed + tap_weights[offset] * padded[:, lead_at : lead_at + local_rows].astype(
            jnp.float32
        )
    return summed


def unfeaturize(gradient, trailing, tap_weights):
    local_rows = gradient.shape[1]
    padded = jnp.concatenate([gradient, trailing], axis=1)
    summed = jnp.zeros(gradient.shape, jnp.float32)
    for offset in range(TAPS):
        summed = summed + tap_weights[offset] * padded[:, offset : offset + local_rows]
    return summed


def to_owners(value, axis):
    count = lax.axis_size(axis)
    batches, rows, channels = value.shape
    split = value.reshape(batches, rows, count, channels // count).transpose(2, 0, 1, 3)
    return lax.all_to_all(split, axis, split_axis=0, concat_axis=0, tiled=True)


def from_owners(value, axis):
    owners, batches, rows, channels = value.shape
    back = lax.all_to_all(value, axis, split_axis=0, concat_axis=0, tiled=True)
    return back.transpose(1, 2, 0, 3).reshape(batches, rows, owners * channels)


def gather_features(value, axis):
    count = lax.axis_size(axis)
    me = lax.axis_index(axis)
    width = value.shape[2]
    gathered = jnp.zeros(value.shape[:2] + (count * width,), value.dtype)
    for step in range(count):
        part = value
        if step:
            pairs = [(source, (source - step) % count) for source in range(count)]
            part = lax.ppermute(value, axis, pairs)
        gathered = lax.dynamic_update_slice_in_dim(
            gathered, part, (me + step) % count * width, 2
        )
    return gathered


def scatter_features(value, axis):
    count = lax.axis_size(axis)
    me = lax.axis_index(axis)
    width = value.shape[2] // count
    total = lax.dynamic_slice_in_dim(value, me * width, width, 2).astype(jnp.float32)
    for step in range(1, count):
        part = lax.dynamic_slice_in_dim(value, (me + step) % count * width, width, 2)
        pairs = [(source, (source + step) % count) for source in range(count)]
        total = total + lax.ppermute(part.astype(jnp.bfloat16), axis, pairs).astype(jnp.float32)
    return total.astype(jnp.bfloat16)


def body(query_in, key_in, value_in, short_filter, long_filter, out_weight, grad_out):
    batches, local_rows, channels = query_in.shape
    context_size = lax.axis_size("context")
    seq_length = local_rows * context_size
    grad_scale = float(batches * seq_length * GROUP) ** (-0.5)
    margin = TAPS - 1
    tap_weights = jnp.repeat(short_filter, GROUP, axis=2)
    last_rows = jnp.stack(
        [
            query_in[:, local_rows - margin :],
            key_in[:, local_rows - margin :],
            value_in[:, local_rows - margin :],
        ]
    )
    before = shifted(last_rows, "context", 1)
    key_feat = featurize(key_in, before[1], tap_weights[1])
    value_feat = featurize(value_in, before[2], tap_weights[2])
    product = (key_feat * value_feat).astype(jnp.bfloat16)
    weight_rows = lax.all_gather(out_weight, "context", axis=0, tiled=True)
    band = make_band(long_filter)
    product_full = to_owners(product, "context")
    grad_full = gather_features(grad_out, "tensor")
    query_feat = featurize(query_in, before[0], tap_weights[0])
    conv_out = from_owners(
        correlation_call(forward_kernel, "conv_forward", band, product_full), "context"
    )
    gated = (query_feat * conv_out.astype(jnp.float32)).astype(jnp.bfloat16)
    gated, weight_rows = lax.optimization_barrier((gated, weight_rows))
    grad_acc = jnp.einsum("blo,oc->blc", grad_full, weight_rows, preferred_element_type=jnp.float32)
    grad_conv = (grad_acc * query_feat).astype(jnp.bfloat16)
    grad_conv_full = to_owners(grad_conv, "context")
    grad_weight = lax.psum_scatter(
        jnp.einsum("blo,blc->oc", grad_full, gated, preferred_element_type=jnp.float32).astype(
            jnp.bfloat16
        ),
        "context",
        scatter_dimension=0,
        tiled=True,
    ).astype(jnp.float32)
    block_out = jnp.einsum("blc,oc->blo", gated, weight_rows, preferred_element_type=jnp.float32)
    mixed_out = scatter_features(block_out, "tensor")
    grad_product = from_owners(
        correlation_call(backward_kernel, "conv_backward", band, grad_conv_full), "context"
    )
    grad_long = long_grad_call(grad_conv_full, product_full, long_filter.shape[0], grad_scale)
    product_grad = grad_product.astype(jnp.float32)
    grad_qfeat = grad_acc * conv_out.astype(jnp.float32)
    grad_kfeat = product_grad * value_feat
    grad_vfeat = product_grad * key_feat
    first_rows = jnp.stack([grad_qfeat[:, :margin], grad_kfeat[:, :margin], grad_vfeat[:, :margin]])
    following = shifted(first_rows.astype(jnp.bfloat16), "context", -1).astype(first_rows.dtype)
    grad_query = unfeaturize(grad_qfeat, following[0], tap_weights[0]).astype(jnp.bfloat16)
    grad_key = unfeaturize(grad_kfeat, following[1], tap_weights[1]).astype(jnp.bfloat16)
    grad_value = unfeaturize(grad_vfeat, following[2], tap_weights[2]).astype(jnp.bfloat16)
    return (mixed_out, grad_query, grad_key, grad_value, grad_weight, grad_long)


def solution(mesh):
    in_specs = (
        P(None, "context", "tensor"),
        P(None, "context", "tensor"),
        P(None, "context", "tensor"),
        P(None, None, "tensor"),
        P(("tensor", "context"), None),
        P("context", "tensor"),
        P(None, "context", "tensor"),
    )
    out_specs = (
        P(None, "context", "tensor"),
        P(None, "context", "tensor"),
        P(None, "context", "tensor"),
        P(None, "context", "tensor"),
        P("context", "tensor"),
        P(("tensor", "context"), None),
    )
    return jax.shard_map(body, mesh=mesh, in_specs=in_specs, out_specs=out_specs, check_vma=False)
```

time: 746 us -> 411 us (0.55); the launches traced: 735 us -> 409 us
  waiting for transfers between devices: 355 us -> 160 us
  matrix products: 172 us -> 31.7 us
  local copies, waits for them, and re-layouts: 113 us -> 34.2 us
  Pallas kernels: 0 us -> 54.7 us
  starting transfers between devices: 21.2 us -> 40.1 us
  other arithmetic: 26.9 us -> 38.8 us
    dot_general x38 -> x2, matrix products: 151 us -> 21.1 us  [the longest x1 13 us: body(): jnp.einsum('blo,oc->blc', grad_full, weight_rows, preferred_element_type=...]
    reduce_scatter x2 -> x1, waiting for transfers between devices: 152 us -> 46.6 us  [body(): lax.psum_scatter(jnp.einsum('blo,blc->oc', grad_full, gated, preferred_el...]
    all_gather x1, waiting for transfers between devices: 129 us -> 25.7 us  [body(): weight_rows = lax.all_gather(out_weight, 'context', axis=0, tiled=True)]
    pallas_call x0 -> x4, Pallas kernels: none -> 54.7 us  [the longest x2 32.9 us: correlation_call(): pl.pallas_call(kernel, out_shape=jax.ShapeDtypeStruct(signal.shape, jnp.b...]
    ppermute x0 -> x2, waiting for transfers between devices: none -> 42.3 us  [the longest x1 22.9 us: scatter_features(): lax.ppermute(part.astype(jnp.bfloat16), axis, pairs).astype(jnp.float32)]
    all_gather x1 -> x0, waiting for transfers between devices: 30.8 us -> none  [body(): grad_full = lax.all_gather(grad_out, 'tensor', axis=2, tiled=True)]
    sub x6 -> x0, local copies, waits for them, and re-layouts: 16.5 us -> none  [the longest x2 11.3 us: complex_product(): first_pair[0] * second_pair[0] - first_pair[1] * second_pair[1]]
    all_to_all x3, starting transfers between devices: 17.4 us -> 33 us  [the longest x2 25.1 us: from_owners(): back = lax.all_to_all(value, axis, split_axis=0, concat_axis=0, tiled=True)]
  transfers between devices with their start and end apart: 9 -> 9, of which waited for: 8 -> 6; matrix products, arithmetic and copies ran while one was open for 11% -> 22% of each run, Pallas kernels for 0% -> 13%
where the time goes in v1:
time: 411 us; the launch traced here: 409 us
  waiting for transfers between devices  160 us (39%)
  Pallas kernels  54.7 us (13%)
  starting transfers between devices  40.1 us (10%)
  other arithmetic  38.8 us (9%)
  blocking collectives  36.2 us (9%)
  local copies, waits for them, and re-layouts  34.2 us (8%)
  matrix products  31.7 us (8%)
  between operations  14.3 us (3%)
    reduce_scatter x1, waiting for transfers between devices, body(): lax.psum_scatter(jnp.einsum('blo,blc->oc', grad_full, gated, preferred_el...  46.6 us
    all_to_all x1, blocking collectives, to_owners(): return lax.all_to_all(split, axis, split_axis=0, concat_axis=0, tiled=True)  36.2 us
    all_to_all x1, waiting for transfers between devices, to_owners(): return lax.all_to_all(split, axis, split_axis=0, concat_axis=0, tiled=True)  34 us
    pallas_call x2, Pallas kernels, correlation_call(): pl.pallas_call(kernel, out_shape=jax.ShapeDtypeStruct(signal.shape, jnp.b...  32.9 us
    all_gather x1, waiting for transfers between devices, body(): weight_rows = lax.all_gather(out_weight, 'context', axis=0, tiled=True)  25.7 us
    all_to_all x2, starting transfers between devices, from_owners(): back = lax.all_to_all(value, axis, split_axis=0, concat_axis=0, tiled=True)  25.1 us
    ppermute x1, waiting for transfers between devices, scatter_features(): lax.ppermute(part.astype(jnp.bfloat16), axis, pairs).astype(jnp.float32)  22.9 us
    ppermute x1, waiting for transfers between devices, gather_features(): part = lax.ppermute(value, axis, pairs)  19.4 us
  transfers between devices with their start and end apart: 9, of which 6 were waited for; matrix products, arithmetic and copies ran while one was open for 22% of the time, Pallas kernels for 13%

profile of v1, /device:TPU:0, one launch (start us, length us, event | category | flops | bytes accessed | tf_op | source)
XLA Modules:
  0.0 409.5 jit_solution(14118159852652913648)
XLA Ops:
  9.8 2.4 collective-permute-start
  16.3 5.0 %multiply_convert_fusion.2 = (bf16[2,128,2048]{2,1,0:T(8,128)(2,1)S(1)}, f32[2,128,2048]{2,1,0:T(8,128)}, f32[2,128,2048]{2,1,0:T(8,128)}) fusion(bf16[2,128,2048]{2,1,0:T(8,128)(2,1)S(1)} %copy-done.3, bf16[2,6,2048]{2,1,0:T(8,128)(2,1)S(1)} %get-tuple-element.23, f32[2048]{0:T(1024)S(1)} %broadcast_in_dim.129, f32[2048]{0:T(1024)S(1)} %broadcast_in_dim.127, ...), kind=kLoop, calls=%fused_computation.107 | loop fusion | flops 40894464 | bytes 7553024 | tf_op jit(solution)/shard_map/convert_element_type | solution.py:311
  23.3 7.8 %all-to-all-start = ((bf16[16,2,128,128]{3,2,1,0:T(8,128)(2,1)}), bf16[16,2,128,128]{3,2,1,0:T(8,128)(2,1)S(1)}, u32[]{:S(2)}, u32[]{:S(2)}) async-start(bf16[16,2,128,128]{3,2,1,0:T(8,128)(2,1)} %bitcast.28), calls=%async_computation | async-start | bytes 2097152 | tf_op jit(solution)/shard_map/all_to_all | solution.py:257
  31.2 5.9 %band.1.band_ref = bf16[8,256,2048]{2,1,0:T(8,128)(2,1)} custom-call(f32[8,2048]{1,0:T(8,128)} %filter_ref.1), custom_call_target="tpu_custom_call" | custom-call | bytes 8388608 | tf_op jit(solution)/shard_map/band/pallas_call | solution.py:46
  37.1 34.0 %all-to-all-done.product_ref = bf16[16,2,128,128]{3,2,1,0:T(8,128)(2,1)S(1)} async-done(((bf16[16,2,128,128]{3,2,1,0:T(8,128)(2,1)}), bf16[16,2,128,128]{3,2,1,0:T(8,128)(2,1)S(1)}, u32[]{:S(2)}, u32[]{:S(2)}) %all-to-all-start) | async-done | bytes 1048608 | tf_op jit(solution)/shard_map/all_to_all | solution.py:257
  72.0 16.7 %conv_forward.1 = bf16[16,2,128,128]{3,2,1,0:T(8,128)(2,1)} custom-call(bf16[8,256,2048]{2,1,0:T(8,128)(2,1)} %band.1.band_ref, bf16[16,2,128,128]{3,2,1,0:T(8,128)(2,1)} %copy-done.5), custom_call_target="tpu_custom_call" | custom-call | flops 8589934592 | bytes 10485760 | tf_op jit(solution)/shard_map/conv_forward/pallas_call | solution.py:188
  88.8 13.1 %all-to-all-start.1 = ((bf16[16,2,128,128]{3,2,1,0:T(8,128)(2,1)}), bf16[16,2,128,128]{3,2,1,0:T(8,128)(2,1)S(1)}, u32[]{:S(2)}, u32[]{:S(2)}) async-start(bf16[16,2,128,128]{3,2,1,0:T(8,128)(2,1)} %conv_forward.1), calls=%async_computation.1 | async-start | bytes 2097152 | tf_op jit(solution)/shard_map/all_to_all | solution.py:262
  103.7 2.3 copy.20
  108.5 19.4 %collective-permute-done.2 = bf16[2,128,2048]{2,1,0:T(8,128)(2,1)} collective-permute-done((bf16[2,128,2048]{2,1,0:T(8,128)(2,1)}, bf16[2,128,2048]{2,1,0:T(8,128)(2,1)}, u32[]{:S(2)}, u32[]{:S(2)}) %collective-permute-start.2) | collective-permute-done | bytes 1048608 | tf_op jit(solution)/shard_map/ppermute | solution.py:275
  127.9 2.3 copy.21
  131.6 10.2 %all-to-all-done.1 = bf16[16,2,128,128]{3,2,1,0:T(8,128)(2,1)S(1)} async-done(((bf16[16,2,128,128]{3,2,1,0:T(8,128)(2,1)}), bf16[16,2,128,128]{3,2,1,0:T(8,128)(2,1)S(1)}, u32[]{:S(2)}, u32[]{:S(2)}) %all-to-all-start.1) | async-done | bytes 1048608 | tf_op jit(solution)/shard_map/all_to_all | solution.py:262
  143.3 2.9 copy.18
  146.2 2.9 copy.19
  149.1 6.9 %multiply_convert_fusion.1 = (bf16[2,128,2048]{2,1,0:T(8,128)(2,1)S(1)}, f32[2,128,2048]{2,1,0:T(8,128)}) fusion(f32[2,128,2048]{2,1,0:T(8,128)} %copy.19, bf16[2,128,2048]{2,1,0:T(8,128)(2,1)} %param.7, bf16[2,6,2048]{2,1,0:T(8,128)(2,1)S(1)} %get-tuple-element.22, f32[2048]{0:T(1024)S(1)} %broadcast_in_dim.101, f32[2048]{0:T(1024)S(1)} %broadcast_in_dim.99, ...), kind=kLoop, calls=%fused_computation.106 | loop fusion | flops 20971520 | bytes 6397952 | tf_op jit(solution)/shard_map/convert_element_type | solution.py:320
  156.0 25.7 %all-gather.2.cloned.1.call-done = bf16[4096,2048]{1,0:T(8,128)(2,1)} async-done(((bf16[256,2048]{1,0:T(8,128)(2,1)}), bf16[4096,2048]{1,0:T(8,128)(2,1)}) %all-gather.2.cloned.1.call-update) | async-done | bytes 16777232 | tf_op jit(solution)/shard_map/all_gather | solution.py:312
  181.8 8.1 %bitcast_convert_fusion = bf16[4096,2048]{1,0:T(8,128)(2,1)} fusion(bf16[2,128,4096]{1,2,0:T(8,128)(2,1)S(1)} %constant_dynamic-update-slice_fusion, bf16[2,128,2048]{2,1,0:T(8,128)(2,1)S(1)} %get-tuple-element.8), kind=kOutput, calls=%fused_computation | convolution fusion | flops 4303355904 | bytes 19922944 | tf_op jit(solution)/shard_map/blo,blc->oc/dot_general | solution.py:326
  189.9 13.0 %fusion.76 = (f32[2,128,2048]{2,1,0:T(8,128)}, bf16[2,128,2048]{2,1,0:T(8,128)(2,1)}) fusion(f32[2,128,2048]{2,1,0:T(8,128)} %copy.19, f32[2,128,2048]{2,1,0:T(8,128)} %get-tuple-element.11, bf16[2,128,4096]{1,2,0:T(8,128)(2,1)S(1)} %constant_dynamic-update-slice_fusion, bf16[4096,2048]{1,0:T(8,128)(2,1)} %all-gather.2.cloned.1.call-done), kind=kOutput, calls=%fused_computation.178 | convolution fusion | flops 4296540160 | bytes 26214400 | tf_op jit(solution)/shard_map/blo,oc->blc/dot_general | solution.py:322
  205.3 36.2 %all_to_all.20.grad_ref = bf16[16,2,128,128]{3,2,1,0:T(8,128)(2,1)} all-to-all(bf16[16,2,128,128]{3,2,1,0:T(8,128)(2,1)S(1)} %bitcast.93), channel_id=1, replica_groups=mesh['context'=16,'tensor'=2] {'context'}, dimensions={0} | all-to-all | bytes 2097152 | tf_op jit(solution)/shard_map/all_to_all | solution.py:257
  241.5 16.2 %conv_backward.1 = bf16[16,2,128,128]{3,2,1,0:T(8,128)(2,1)} custom-call(bf16[8,256,2048]{2,1,0:T(8,128)(2,1)} %band.1.band_ref, bf16[16,2,128,128]{3,2,1,0:T(8,128)(2,1)} %all_to_all.20.grad_ref), custom_call_target="tpu_custom_call" | custom-call | flops 8589934592 | bytes 10485760 | tf_op jit(solution)/shard_map/conv_backward/pallas_call | solution.py:188
  257.7 12.1 %all-to-all-start.3 = ((bf16[16,2,128,128]{3,2,1,0:T(8,128)(2,1)}), bf16[16,2,128,128]{3,2,1,0:T(8,128)(2,1)}, u32[]{:S(2)}, u32[]{:S(2)}) async-start(bf16[16,2,128,128]{3,2,1,0:T(8,128)(2,1)} %conv_backward.1), calls=%async_computation.3 | async-start | bytes 2097152 | tf_op jit(solution)/shard_map/all_to_all | solution.py:262
  269.7 10.6 %fusion.2 = f32[2,128,4096]{2,1,0:T(8,128)} fusion(bf16[2,128,2048]{2,1,0:T(8,128)(2,1)S(1)} %get-tuple-element.8, bf16[4096,2048]{1,0:T(8,128)(2,1)} %all-gather.2.cloned.1.call-done), kind=kOutput, calls=%fused_computation.3 | convolution fusion | flops 4294967296 | bytes 22020096 | tf_op jit(solution)/shard_map/blc,oc->blo/dot_general | solution.py:333
  284.6 22.9 %collective-permute-done.1 = bf16[2,128,2048]{2,1,0:T(8,128)(2,1)S(1)} collective-permute-done((bf16[2,128,2048]{2,1,0:T(8,128)(2,1)S(1)}, bf16[2,128,2048]{2,1,0:T(8,128)(2,1)S(1)}, u32[]{:S(2)}, u32[]{:S(2)}) %collective-permute-start.1) | collective-permute-done | bytes 1048608 | tf_op jit(solution)/shard_map/ppermute | solution.py:290
  307.5 2.9 add_convert_fusion
  311.8 1.9 copy.26
  313.7 2.9 copy.27
  316.6 3.6 fusion.77
  322.9 15.9 %long_grad.1 = f32[8,2048]{1,0:T(8,128)} custom-call(bf16[16,2,128,128]{3,2,1,0:T(8,128)(2,1)} %all_to_all.20.grad_ref, bf16[16,2,128,128]{3,2,1,0:T(8,128)(2,1)} %copy-done.5), custom_call_target="tpu_custom_call" | custom-call | flops 8589934592 | bytes 2162688 | tf_op jit(solution)/shard_map/long_grad/pallas_call | solution.py:212
  338.8 8.5 %fusion.42 = bf16[2,128,2048]{2,1,0:T(8,128)(2,1)} fusion(f32[2,6,2048]{2,1,0:T(8,128)S(1)} %get-tuple-element.21, f32[2,128,2048]{2,1,0:T(8,128)} %get-tuple-element.15, f32[2048]{0:T(1024)S(1)} %broadcast_in_dim.101, f32[2048]{0:T(1024)S(1)} %broadcast_in_dim.99, f32[2048]{0:T(1024)S(1)} %broadcast_in_dim.97, f32[2048]{0:T(1024)S(1)} %broadcast_in_dim.95, ...), kind=kLoop, calls=%fused_computation.73 | loop fusion | flops 10485760 | bytes 3301376 | tf_op jit(solution)/shard_map/convert_element_type | solution.py:345
  347.3 3.0 fusion.25
  350.3 3.0 fusion.8
  353.3 46.6 %reduce-scatter.2.cloned.1.call-done = bf16[256,2048]{1,0:T(8,128)(2,1)} async-done(((bf16[4096,2048]{1,0:T(8,128)(2,1)}), bf16[256,2048]{1,0:T(8,128)(2,1)}) %reduce-scatter.2.cloned.1.call-update) | async-done | bytes 1048592 | tf_op jit(solution)/shard_map/reduce_scatter | solution.py:325
  399.8 2.8 convert_element_type.157
  (86 shorter events, 27.6 us)
Async XLA Ops:
  7.2 9.1 %copy-start.3 = (bf16[2,128,2048]{2,1,0:T(8,128)(2,1)S(1)}, bf16[2,128,2048]{2,1,0:T(8,128)(2,1)}, u32[]{:S(2)}) copy-start(bf16[2,128,2048]{2,1,0:T(8,128)(2,1)} %param.9) | copy-start | bytes 3145732
  7.2 9.1 %copy-start.4 = (bf16[2,128,2048]{2,1,0:T(8,128)(2,1)S(1)}, bf16[2,128,2048]{2,1,0:T(8,128)(2,1)}, u32[]{:S(2)}) copy-start(bf16[2,128,2048]{2,1,0:T(8,128)(2,1)} %param.8) | copy-start | bytes 3145732
  7.2 174.6 %all-gather.2.cloned.1.call-start = ((), (), s32[]{:S(2)}) async-start(), calls=%async_computation.5 | async-start | bytes 17825792 | tf_op jit(solution)/shard_map/all_gather | solution.py:312
  9.8 6.5 %collective-permute-start = (bf16[3,2,6,2048]{3,2,1,0:T(8,128)(2,1)S(1)}, bf16[3,2,6,2048]{3,2,1,0:T(8,128)(2,1)S(1)}, u32[]{:S(2)}, u32[]{:S(2)}) collective-permute-start(bf16[3,2,6,2048]{3,2,1,0:T(8,128)(2,1)S(1)} %pad_maximum_fusion.6), channel_id=1, source_target_pairs={{0,2},{2,4},{4,6},{6,8},{8,10},{10,12},{12,14},{14,16},{16,18},{18... | collective-permute-start | bytes 442376 | tf_op jit(solution)/shard_map/ppermute | solution.py:20
  23.3 47.8 %all-to-all-start = ((bf16[16,2,128,128]{3,2,1,0:T(8,128)(2,1)}), bf16[16,2,128,128]{3,2,1,0:T(8,128)(2,1)S(1)}, u32[]{:S(2)}, u32[]{:S(2)}) async-start(bf16[16,2,128,128]{3,2,1,0:T(8,128)(2,1)} %bitcast.28), calls=%async_computation | async-start | bytes 2097152 | tf_op jit(solution)/shard_map/all_to_all | solution.py:257
  71.1 1.0 copy-start.5
  88.8 53.0 %all-to-all-start.1 = ((bf16[16,2,128,128]{3,2,1,0:T(8,128)(2,1)}), bf16[16,2,128,128]{3,2,1,0:T(8,128)(2,1)S(1)}, u32[]{:S(2)}, u32[]{:S(2)}) async-start(bf16[16,2,128,128]{3,2,1,0:T(8,128)(2,1)} %conv_forward.1), calls=%async_computation.1 | async-start | bytes 2097152 | tf_op jit(solution)/shard_map/all_to_all | solution.py:262
  101.8 298.0 %reduce-scatter.2.cloned.1.call-start = ((), (), s32[]{:S(2)}) async-start(), calls=%async_computation.6 | async-start | bytes 17825792 | tf_op jit(solution)/shard_map/reduce_scatter | solution.py:325
  102.1 25.9 %collective-permute-start.2 = (bf16[2,128,2048]{2,1,0:T(8,128)(2,1)}, bf16[2,128,2048]{2,1,0:T(8,128)(2,1)}, u32[]{:S(2)}, u32[]{:S(2)}) collective-permute-start(bf16[2,128,2048]{2,1,0:T(8,128)(2,1)} %param.13), channel_id=1, source_target_pairs={{0,1},{1,0},{2,3},{3,2},{4,5},{5,4},{6,7},{7,6},{8,9},{9,8},{10,11... | collective-permute-start | bytes 3145736 | tf_op jit(solution)/shard_map/ppermute | solution.py:275
  107.1 1.2 copy-start.2
  257.7 52.7 %all-to-all-start.3 = ((bf16[16,2,128,128]{3,2,1,0:T(8,128)(2,1)}), bf16[16,2,128,128]{3,2,1,0:T(8,128)(2,1)}, u32[]{:S(2)}, u32[]{:S(2)}) async-start(bf16[16,2,128,128]{3,2,1,0:T(8,128)(2,1)} %conv_backward.1), calls=%async_computation.3 | async-start | bytes 2097152 | tf_op jit(solution)/shard_map/all_to_all | solution.py:262
  282.1 25.4 %collective-permute-start.1 = (bf16[2,128,2048]{2,1,0:T(8,128)(2,1)S(1)}, bf16[2,128,2048]{2,1,0:T(8,128)(2,1)S(1)}, u32[]{:S(2)}, u32[]{:S(2)}) collective-permute-start(bf16[2,128,2048]{2,1,0:T(8,128)(2,1)S(1)} %dynamic-slice_convert_fusion), channel_id=1, source_target_pairs={{0,1},{1,0},{2,3},{3,2},{4,5},{5,4},{6,7},{7,6},{8,9},{9,8},{10,11... | collective-permute-start | bytes 3145736 | tf_op jit(solution)/shard_map/ppermute | solution.py:290
  320.2 1.3 copy-start
  321.6 17.2 %collective-permute-start.3 = (bf16[3,2,6,2048]{3,2,1,0:T(8,128)(2,1)S(1)}, bf16[3,2,6,2048]{3,2,1,0:T(8,128)(2,1)S(1)}, u32[]{:S(2)}, u32[]{:S(2)}) collective-permute-start(bf16[3,2,6,2048]{3,2,1,0:T(8,128)(2,1)S(1)} %pad_maximum_fusion.7), channel_id=1, source_target_pairs={{2,0},{4,2},{6,4},{8,6},{10,8},{12,10},{14,12},{16,14},{18,16},{20... | collective-permute-start | bytes 442376 | tf_op jit(solution)/shard_map/ppermute | solution.py:20
  338.8 8.5 %copy-start.1 = (f32[2,128,2048]{2,1,0:T(8,128)S(1)}, f32[2,128,2048]{2,1,0:T(8,128)}, u32[]{:S(2)}) copy-start(f32[2,128,2048]{2,1,0:T(8,128)} %copy-done) | copy-start | bytes 6291460
Sparse Core Ops, SparseCore 0:
  10.2 171.5 all-gather.1
  190.0 209.8 reduce-scatter.1

commit v2 on v1

--- a/solution.py
+++ b/solution.py
@@ -291,6 +291,66 @@
     return total.astype(jnp.bfloat16)
 
 
+def ring_order(chips):
+    return list(range(0, chips, 2)) + list(range(chips - 1, 0, -2))
+
+
+def ring_pairs(order, step):
+    chips = len(order)
+    return [
+        (2 * order[k] + core, 2 * order[(k + step) % chips] + core)
+        for k in range(chips)
+        for core in range(2)
+    ]
+
+
+def scattered_weight_grad(grad_full, gated, axis):
+    count = lax.axis_size(axis)
+    chips = count // 2
+    order = ring_order(chips)
+    me = lax.axis_index(axis)
+    core = me % 2
+    place = jnp.array([order.index(chip) for chip in range(chips)], jnp.int32)[me // 2]
+    order_table = jnp.array(order, jnp.int32)
+    rows = grad_full.shape[2] // count
+    half = gated.shape[2] // 2
+    halves = (gated[:, :, :half], gated[:, :, half:])
+    siblings = [(device, device ^ 1) for device in range(count)]
+
+    def partial_sum(position, owner_core, side):
+        owner = 2 * order_table[position % chips] + owner_core
+        columns = lax.dynamic_slice_in_dim(grad_full, owner * rows, rows, 2)
+        return jnp.einsum(
+            "blo,blc->oc", columns, halves[side], preferred_element_type=jnp.float32
+        )
+
+    def positions(step):
+        return (place - 1 - step, place + 1 + step)
+
+    received = []
+    for step in range(chips):
+        sent = jnp.stack(
+            [
+                partial_sum(positions(step)[side], 1 - core, side).astype(jnp.bfloat16)
+                for side in range(2)
+            ]
+        )
+        received.append(lax.ppermute(sent, axis, siblings))
+    travelling = [None, None]
+    for step in range(chips):
+        for side in range(2):
+            total = partial_sum(positions(step)[side], core, side)
+            total = total + received[step][side].astype(jnp.float32)
+            if step:
+                total = total + travelling[side].astype(jnp.float32)
+            if step < chips - 1:
+                total = lax.ppermute(
+                    total.astype(jnp.bfloat16), axis, ring_pairs(order, 1 - 2 * side)
+                )
+            travelling[side] = total
+    return jnp.concatenate(travelling, axis=1)
+
+
 def body(query_in, key_in, value_in, short_filter, long_filter, out_weight, grad_out):
     batches, local_rows, channels = query_in.shape
     context_size = lax.axis_size("context")
@@ -313,6 +373,7 @@
     band = make_band(long_filter)
     product_full = to_owners(product, "context")
     grad_full = gather_features(grad_out, "tensor")
+    product_full, grad_full = lax.optimization_barrier((product_full, grad_full))
     query_feat = featurize(query_in, before[0], tap_weights[0])
     conv_out = from_owners(
         correlation_call(forward_kernel, "conv_forward", band, product_full), "context"
@@ -321,15 +382,9 @@
     gated, weight_rows = lax.optimization_barrier((gated, weight_rows))
     grad_acc = jnp.einsum("blo,oc->blc", grad_full, weight_rows, preferred_element_type=jnp.float32)
     grad_conv = (grad_acc * query_feat).astype(jnp.bfloat16)
+    grad_conv, gated = lax.optimization_barrier((grad_conv, gated))
     grad_conv_full = to_owners(grad_conv, "context")
-    grad_weight = lax.psum_scatter(
-        jnp.einsum("blo,blc->oc", grad_full, gated, preferred_element_type=jnp.float32).astype(
-            jnp.bfloat16
-        ),
-        "context",
-        scatter_dimension=0,
-        tiled=True,
-    ).astype(jnp.float32)
+    grad_weight = scattered_weight_grad(grad_full, gated, "context")
     block_out = jnp.einsum("blc,oc->blo", gated, weight_rows, preferred_element_type=jnp.float32)
     mixed_out = scatter_features(block_out, "tensor")
     grad_product = from_owners(

time: 411 us -> 411 us (level)
  blocking collectives: 36.2 us -> 0 us
  waiting for transfers between devices: 160 us -> 131 us
  starting transfers between devices: 40.1 us -> 67 us
  between operations: 14.3 us -> 35.4 us
  matrix products: 31.7 us -> 49.2 us
    ppermute x0 -> x22, waiting for transfers between devices: none -> 58.6 us  [the longest x14 58.5 us: scattered_weight_grad(): lax.ppermute(total.astype(jnp.bfloat16), axis, ring_pairs(order, 1 - 2 *...]
    reduce_scatter x1 -> x0, waiting for transfers between devices: 46.6 us -> none  [body(): lax.psum_scatter(jnp.einsum('blo,blc->oc', grad_full, gated, preferred_el...]
    all_to_all x1 -> x0, blocking collectives: 36.2 us -> none  [to_owners(): return lax.all_to_all(split, axis, split_axis=0, concat_axis=0, tiled=True)]
    ppermute x0 -> x22, starting transfers between devices: none -> 29.1 us  [the longest x14 27.3 us: scattered_weight_grad(): lax.ppermute(total.astype(jnp.bfloat16), axis, ring_pairs(order, 1 - 2 *...]
    ppermute x1, waiting for transfers between devices: 22.9 us -> 0.01 us  [scatter_features(): lax.ppermute(part.astype(jnp.bfloat16), axis, pairs).astype(jnp.float32)]
    all_to_all x1 -> x2, waiting for transfers between devices: 34 us -> 12.4 us  [to_owners(): return lax.all_to_all(split, axis, split_axis=0, concat_axis=0, tiled=True)]
    dot_general x1 -> x32, matrix products: 8.09 us -> 26.7 us  [partial_sum(): jnp.einsum('blo,blc->oc', columns, halves[side], preferred_element_type=j...]
    all_to_all x2, starting transfers between devices: 25.1 us -> 17.8 us  [from_owners(): back = lax.all_to_all(value, axis, split_axis=0, concat_axis=0, tiled=True)]
  transfers between devices with their start and end apart: 9 -> 31, of which waited for: 6 -> 10; matrix products, arithmetic and copies ran while one was open for 22% -> 23% of each run, Pallas kernels for 13% -> 13%
where the time goes in v2:
time: 411 us; the launch traced here: 409 us
  waiting for transfers between devices  131 us (32%)
  starting transfers between devices  67 us (16%)
  Pallas kernels  54.6 us (13%)
  matrix products  49.2 us (12%)
  other arithmetic  38.7 us (9%)
  between operations  35.4 us (9%)
  local copies, waits for them, and re-layouts  32.7 us (8%)
    ppermute x14, waiting for transfers between devices, scattered_weight_grad(): lax.ppermute(total.astype(jnp.bfloat16), axis, ring_pairs(order, 1 - 2 *...  58.5 us
    pallas_call x2, Pallas kernels, correlation_call(): pl.pallas_call(kernel, out_shape=jax.ShapeDtypeStruct(signal.shape, jnp.b...  32.9 us
    ppermute x14, starting transfers between devices, scattered_weight_grad(): lax.ppermute(total.astype(jnp.bfloat16), axis, ring_pairs(order, 1 - 2 *...  27.3 us
    dot_general x32, matrix products, partial_sum(): jnp.einsum('blo,blc->oc', columns, halves[side], preferred_element_type=j...  26.7 us
    all_gather x1, waiting for transfers between devices, body(): weight_rows = lax.all_gather(out_weight, 'context', axis=0, tiled=True)  26.3 us
    all_to_all x2, starting transfers between devices, from_owners(): back = lax.all_to_all(value, axis, split_axis=0, concat_axis=0, tiled=True)  17.8 us
    ppermute x1, waiting for transfers between devices, gather_features(): part = lax.ppermute(value, axis, pairs)  17.6 us
    all_to_all x2, waiting for transfers between devices, from_owners(): back = lax.all_to_all(value, axis, split_axis=0, concat_axis=0, tiled=True)  15.8 us
  transfers between devices with their start and end apart: 31, of which 10 were waited for; matrix products, arithmetic and copies ran while one was open for 23% of the time, Pallas kernels for 13%

profile of v2, /device:TPU:0, one launch (start us, length us, event | category | flops | bytes accessed | tf_op | source)
XLA Modules:
  0.0 409.0 jit_solution(11573908629291638338)
XLA Ops:
  15.6 5.0 %multiply_convert_fusion.2 = (bf16[2,128,2048]{2,1,0:T(8,128)(2,1)S(1)}, f32[2,128,2048]{2,1,0:T(8,128)}, f32[2,128,2048]{2,1,0:T(8,128)}) fusion(bf16[2,128,2048]{2,1,0:T(8,128)(2,1)S(1)} %copy-done.2, bf16[2,6,2048]{2,1,0:T(8,128)(2,1)S(1)} %get-tuple-element.31, f32[2048]{0:T(1024)S(1)} %broadcast_in_dim.115, f32[2048]{0:T(1024)S(1)} %broadcast_in_dim.113, ...), kind=kLoop, calls=%fused_computation.108 | loop fusion | flops 40894464 | bytes 7553024 | tf_op jit(solution)/shard_map/convert_element_type | solution.py:371
  22.6 8.7 %all-to-all-start = ((bf16[16,2,128,128]{3,2,1,0:T(8,128)(2,1)}), bf16[16,2,128,128]{3,2,1,0:T(8,128)(2,1)}, u32[]{:S(2)}, u32[]{:S(2)}) async-start(bf16[16,2,128,128]{3,2,1,0:T(8,128)(2,1)} %bitcast.20), calls=%async_computation | async-start | bytes 2097152 | tf_op jit(solution)/shard_map/all_to_all | solution.py:257
  33.5 6.0 %band.1.band_ref = bf16[8,256,2048]{2,1,0:T(8,128)(2,1)} custom-call(f32[8,2048]{1,0:T(8,128)} %filter_ref.1), custom_call_target="tpu_custom_call" | custom-call | bytes 8388608 | tf_op jit(solution)/shard_map/band/pallas_call | solution.py:46
  39.9 17.6 %collective-permute-done.1 = bf16[2,128,2048]{1,2,0:T(8,128)(2,1)} collective-permute-done((bf16[2,128,2048]{1,2,0:T(8,128)(2,1)S(1)}, bf16[2,128,2048]{1,2,0:T(8,128)(2,1)}, u32[]{:S(2)}, u32[]{:S(2)}) %collective-permute-start.1) | collective-permute-done | bytes 1048608 | tf_op jit(solution)/shard_map/ppermute | solution.py:275
  58.8 12.4 %all-to-all-done.product_ref = bf16[16,2,128,128]{3,2,1,0:T(8,128)(2,1)} async-done(((bf16[16,2,128,128]{3,2,1,0:T(8,128)(2,1)}), bf16[16,2,128,128]{3,2,1,0:T(8,128)(2,1)}, u32[]{:S(2)}, u32[]{:S(2)}) %all-to-all-start) | async-done | bytes 1048608 | tf_op jit(solution)/shard_map/all_to_all | solution.py:257
  71.2 16.8 %conv_forward.1 = bf16[16,2,128,128]{3,2,1,0:T(8,128)(2,1)} custom-call(bf16[8,256,2048]{2,1,0:T(8,128)(2,1)} %band.1.band_ref, bf16[16,2,128,128]{3,2,1,0:T(8,128)(2,1)} %all-to-all-done.product_ref), custom_call_target="tpu_custom_call" | custom-call | flops 8589934592 | bytes 10485760 | tf_op jit(solution)/shard_map/conv_forward/pallas_call | solution.py:188
  88.0 13.2 %all-to-all-start.1 = ((bf16[16,2,128,128]{3,2,1,0:T(8,128)(2,1)}), bf16[16,2,128,128]{3,2,1,0:T(8,128)(2,1)S(1)}, u32[]{:S(2)}, u32[]{:S(2)}) async-start(bf16[16,2,128,128]{3,2,1,0:T(8,128)(2,1)} %conv_forward.1), calls=%async_computation.1 | async-start | bytes 2097152 | tf_op jit(solution)/shard_map/all_to_all | solution.py:262
  125.3 15.8 %all-to-all-done.1 = bf16[16,2,128,128]{3,2,1,0:T(8,128)(2,1)S(1)} async-done(((bf16[16,2,128,128]{3,2,1,0:T(8,128)(2,1)}), bf16[16,2,128,128]{3,2,1,0:T(8,128)(2,1)S(1)}, u32[]{:S(2)}, u32[]{:S(2)}) %all-to-all-start.1) | async-done | bytes 1048608 | tf_op jit(solution)/shard_map/all_to_all | solution.py:262
  145.6 2.9 copy.23
  148.6 6.9 %multiply_convert_fusion.1 = (bf16[2,128,2048]{2,1,0:T(8,128)(2,1)S(1)}, f32[2,128,2048]{2,1,0:T(8,128)}) fusion(f32[2,128,2048]{2,1,0:T(8,128)} %copy.23, bf16[2,128,2048]{2,1,0:T(8,128)(2,1)} %param.9, bf16[2,6,2048]{2,1,0:T(8,128)(2,1)S(1)} %get-tuple-element.30, f32[2048]{0:T(1024)S(1)} %broadcast_in_dim.130, f32[2048]{0:T(1024)S(1)} %broadcast_in_dim.128, ...), kind=kLoop, calls=%fused_computation.106 | loop fusion | flops 20971520 | bytes 6397952 | tf_op jit(solution)/shard_map/convert_element_type | solution.py:381
  155.5 26.3 %all-gather.2.cloned.1.call-done = bf16[4096,2048]{1,0:T(8,128)(2,1)} async-done(((bf16[256,2048]{1,0:T(8,128)(2,1)}), bf16[4096,2048]{1,0:T(8,128)(2,1)}) %all-gather.2.cloned.1.call-update) | async-done | bytes 16777232 | tf_op jit(solution)/shard_map/all_gather | solution.py:372
  181.8 12.3 %fusion.264 = (f32[2,128,2048]{2,1,0:T(8,128)}, bf16[2,128,2048]{2,1,0:T(8,128)(2,1)}) fusion(f32[2,128,2048]{2,1,0:T(8,128)} %copy.23, f32[2,128,2048]{2,1,0:T(8,128)} %get-tuple-element.19, bf16[2,128,4096]{1,2,0:T(8,128)(2,1)S(1)} %constant_dynamic-update-slice_fusion, bf16[4096,2048]{1,0:T(8,128)(2,1)} %all-gather.2.cloned.1.call-done), kind=kOutput, calls=%fused_computation.406 | convolution fusion | flops 4296540160 | bytes 26214400 | tf_op jit(solution)/shard_map/blo,oc->blc/dot_general | solution.py:383
  194.1 10.2 %fusion = f32[2,128,4096]{2,1,0:T(8,128)} fusion(bf16[2,128,2048]{2,1,0:T(8,128)(2,1)S(1)} %get-tuple-element.16, bf16[4096,2048]{1,0:T(8,128)(2,1)} %all-gather.2.cloned.1.call-done), kind=kOutput, calls=%fused_computation | convolution fusion | flops 4294967296 | bytes 22020096 | tf_op jit(solution)/shard_map/blc,oc->blo/dot_general | solution.py:388
  213.0 4.6 %all-to-all-start.2 = ((bf16[16,2,128,128]{3,2,1,0:T(8,128)(2,1)}), bf16[16,2,128,128]{3,2,1,0:T(8,128)(2,1)}, u32[]{:S(2)}, u32[]{:S(2)}) async-start(bf16[16,2,128,128]{3,2,1,0:T(8,128)(2,1)} %bitcast.391), calls=%async_computation.2 | async-start | bytes 2097152 | tf_op jit(solution)/shard_map/all_to_all | solution.py:257
  231.0 17.4 %collective-permute-done.19 = bf16[256,1024]{1,0:T(8,128)(2,1)S(1)} collective-permute-done((bf16[256,1024]{1,0:T(8,128)(2,1)S(1)}, bf16[256,1024]{1,0:T(8,128)(2,1)S(1)}, u32[]{:S(2)}, u32[]{:S(2)}) %collective-permute-start.19) | collective-permute-done | bytes 524320 | tf_op jit(solution)/shard_map/ppermute | solution.py:347
  252.1 7.2 %collective-permute-start.13 = (bf16[256,1024]{1,0:T(8,128)(2,1)}, bf16[256,1024]{1,0:T(8,128)(2,1)}, u32[]{:S(2)}, u32[]{:S(2)}) collective-permute-start(bf16[256,1024]{1,0:T(8,128)(2,1)} %fusion.121), channel_id=1, source_target_pairs={{0,8},{2,10},{8,16},{10,18},{16,24},{18,26},{24,28},{26,30},{28,20... | collective-permute-start | bytes 1572872 | tf_op jit(solution)/shard_map/ppermute | solution.py:347
  259.3 8.3 %collective-permute-done.20 = bf16[256,1024]{1,0:T(8,128)(2,1)S(1)} collective-permute-done((bf16[256,1024]{1,0:T(8,128)(2,1)S(1)}, bf16[256,1024]{1,0:T(8,128)(2,1)S(1)}, u32[]{:S(2)}, u32[]{:S(2)}) %collective-permute-start.20) | collective-permute-done | bytes 524320 | tf_op jit(solution)/shard_map/ppermute | solution.py:347
  268.8 16.1 %conv_backward.1 = bf16[16,2,128,128]{3,2,1,0:T(8,128)(2,1)} custom-call(bf16[8,256,2048]{2,1,0:T(8,128)(2,1)} %band.1.band_ref, bf16[16,2,128,128]{3,2,1,0:T(8,128)(2,1)} %all-to-all-done.2.grad_ref), custom_call_target="tpu_custom_call" | custom-call | flops 8589934592 | bytes 10485760 | tf_op jit(solution)/shard_map/conv_backward/pallas_call | solution.py:188
  284.9 4.7 %all-to-all-start.3 = ((bf16[16,2,128,128]{3,2,1,0:T(8,128)(2,1)}), bf16[16,2,128,128]{3,2,1,0:T(8,128)(2,1)}, u32[]{:S(2)}, u32[]{:S(2)}) async-start(bf16[16,2,128,128]{3,2,1,0:T(8,128)(2,1)} %conv_backward.1), calls=%async_computation.3 | async-start | bytes 2097152 | tf_op jit(solution)/shard_map/all_to_all | solution.py:262
  298.1 20.8 %collective-permute-done.14 = bf16[256,1024]{1,0:T(8,128)(2,1)S(1)} collective-permute-done((bf16[256,1024]{1,0:T(8,128)(2,1)S(1)}, bf16[256,1024]{1,0:T(8,128)(2,1)S(1)}, u32[]{:S(2)}, u32[]{:S(2)}) %collective-permute-start.14) | collective-permute-done | bytes 524320 | tf_op jit(solution)/shard_map/ppermute | solution.py:347
  320.2 7.2 %collective-permute-start.15 = (bf16[256,1024]{1,0:T(8,128)(2,1)S(1)}, bf16[256,1024]{1,0:T(8,128)(2,1)}, u32[]{:S(2)}, u32[]{:S(2)}) collective-permute-start(bf16[256,1024]{1,0:T(8,128)(2,1)S(1)} %fusion.125), channel_id=1, source_target_pairs={{0,8},{2,10},{8,16},{10,18},{16,24},{18,26},{24,28},{26,30},{28,20... | collective-permute-start | bytes 1572872 | tf_op jit(solution)/shard_map/ppermute | solution.py:347
  329.6 15.8 %long_grad.1 = f32[8,2048]{1,0:T(8,128)} custom-call(bf16[16,2,128,128]{3,2,1,0:T(8,128)(2,1)} %all-to-all-done.2.grad_ref, bf16[16,2,128,128]{3,2,1,0:T(8,128)(2,1)} %all-to-all-done.product_ref), custom_call_target="tpu_custom_call" | custom-call | flops 8589934592 | bytes 2162688 | tf_op jit(solution)/shard_map/long_grad/pallas_call | solution.py:212
  356.2 2.9 copy.28
  359.1 2.9 copy.29
  362.1 3.5 fusion.265
  368.6 3.4 collective-permute-start.17
  372.1 3.0 fusion.42
  375.1 3.0 fusion.25
  381.2 3.3 collective-permute-done.17
  386.2 3.0 fusion.8
  389.2 4.5 %collective-permute-done.25 = bf16[256,1024]{1,0:T(8,128)(2,1)S(1)} collective-permute-done((bf16[256,1024]{1,0:T(8,128)(2,1)S(1)}, bf16[256,1024]{1,0:T(8,128)(2,1)S(1)}, u32[]{:S(2)}, u32[]{:S(2)}) %collective-permute-start.25) | collective-permute-done | bytes 524320 | tf_op jit(solution)/shard_map/ppermute | solution.py:347
  395.1 4.2 %collective-permute-done.18 = bf16[256,1024]{1,0:T(8,128)(2,1)S(1)} collective-permute-done((bf16[256,1024]{1,0:T(8,128)(2,1)S(1)}, bf16[256,1024]{1,0:T(8,128)(2,1)S(1)}, u32[]{:S(2)}, u32[]{:S(2)}) %collective-permute-start.18) | collective-permute-done | bytes 524320 | tf_op jit(solution)/shard_map/ppermute | solution.py:347
  (172 shorter events, 83.8 us)
Async XLA Ops:
  7.2 174.6 %all-gather.2.cloned.1.call-start = ((), (), s32[]{:S(2)}) async-start(), calls=%async_computation.4 | async-start | bytes 17825792 | tf_op jit(solution)/shard_map/all_gather | solution.py:372
  9.8 5.8 %collective-permute-start = (bf16[3,2,6,2048]{3,2,1,0:T(8,128)(2,1)S(1)}, bf16[3,2,6,2048]{3,2,1,0:T(8,128)(2,1)S(1)}, u32[]{:S(2)}, u32[]{:S(2)}) collective-permute-start(bf16[3,2,6,2048]{3,2,1,0:T(8,128)(2,1)S(1)} %pad_maximum_fusion.15), channel_id=1, source_target_pairs={{0,2},{2,4},{4,6},{6,8},{8,10},{10,12},{12,14},{14,16},{16,18},{18... | collective-permute-start | bytes 442376 | tf_op jit(solution)/shard_map/ppermute | solution.py:20
  22.6 48.6 %all-to-all-start = ((bf16[16,2,128,128]{3,2,1,0:T(8,128)(2,1)}), bf16[16,2,128,128]{3,2,1,0:T(8,128)(2,1)}, u32[]{:S(2)}, u32[]{:S(2)}) async-start(bf16[16,2,128,128]{3,2,1,0:T(8,128)(2,1)} %bitcast.20), calls=%async_computation | async-start | bytes 2097152 | tf_op jit(solution)/shard_map/all_to_all | solution.py:257
  31.9 25.6 %collective-permute-start.1 = (bf16[2,128,2048]{1,2,0:T(8,128)(2,1)S(1)}, bf16[2,128,2048]{1,2,0:T(8,128)(2,1)}, u32[]{:S(2)}, u32[]{:S(2)}) collective-permute-start(bf16[2,128,2048]{1,2,0:T(8,128)(2,1)S(1)} %copy.20), channel_id=1, source_target_pairs={{0,1},{1,0},{2,3},{3,2},{4,5},{5,4},{6,7},{7,6},{8,9},{9,8},{10,11... | collective-permute-start | bytes 3145736 | tf_op jit(solution)/shard_map/ppermute | solution.py:275
  88.0 24.5 %copy-start.6 = (s32[8]{0:T(128)S(1)}, s32[8]{0:T(128)}, u32[]{:S(2)}) copy-start(s32[8]{0:T(128)} %constant.234.clone) | copy-start | bytes 100
  88.0 53.1 %all-to-all-start.1 = ((bf16[16,2,128,128]{3,2,1,0:T(8,128)(2,1)}), bf16[16,2,128,128]{3,2,1,0:T(8,128)(2,1)S(1)}, u32[]{:S(2)}, u32[]{:S(2)}) async-start(bf16[16,2,128,128]{3,2,1,0:T(8,128)(2,1)} %conv_forward.1), calls=%async_computation.1 | async-start | bytes 2097152 | tf_op jit(solution)/shard_map/all_to_all | solution.py:262
  207.0 88.4 %collective-permute-start.2 = (bf16[2,128,2048]{2,1,0:T(8,128)(2,1)}, bf16[2,128,2048]{2,1,0:T(8,128)(2,1)}, u32[]{:S(2)}, u32[]{:S(2)}) collective-permute-start(bf16[2,128,2048]{2,1,0:T(8,128)(2,1)} %dynamic-slice_convert_fusion), channel_id=1, source_target_pairs={{0,1},{1,0},{2,3},{3,2},{4,5},{5,4},{6,7},{7,6},{8,9},{9,8},{10,11... | collective-permute-start | bytes 3145736 | tf_op jit(solution)/shard_map/ppermute | solution.py:290
  213.0 55.8 %all-to-all-start.2 = ((bf16[16,2,128,128]{3,2,1,0:T(8,128)(2,1)}), bf16[16,2,128,128]{3,2,1,0:T(8,128)(2,1)}, u32[]{:S(2)}, u32[]{:S(2)}) async-start(bf16[16,2,128,128]{3,2,1,0:T(8,128)(2,1)} %bitcast.391), calls=%async_computation.2 | async-start | bytes 2097152 | tf_op jit(solution)/shard_map/all_to_all | solution.py:257
  218.3 8.5 %collective-permute-start.11 = (bf16[2,256,1024]{2,1,0:T(8,128)(2,1)S(1)}, bf16[2,256,1024]{2,1,0:T(8,128)(2,1)S(1)}, u32[]{:S(2)}, u32[]{:S(2)}) collective-permute-start(bf16[2,256,1024]{2,1,0:T(8,128)(2,1)S(1)} %pad_maximum_fusion.14), channel_id=1, source_target_pairs={{0,2},{2,0},{4,6},{6,4},{8,10},{10,8},{12,14},{14,12},{16,18},{18,... | collective-permute-start | bytes 3145736 | tf_op jit(solution)/shard_map/ppermute | solution.py:338
  219.1 11.3 %collective-permute-start.10 = (bf16[2,256,1024]{2,1,0:T(8,128)(2,1)S(1)}, bf16[2,256,1024]{2,1,0:T(8,128)(2,1)S(1)}, u32[]{:S(2)}, u32[]{:S(2)}) collective-permute-start(bf16[2,256,1024]{2,1,0:T(8,128)(2,1)S(1)} %pad_maximum_fusion.13), channel_id=1, source_target_pairs={{0,2},{2,0},{4,6},{6,4},{8,10},{10,8},{12,14},{14,12},{16,18},{18,... | collective-permute-start | bytes 3145736 | tf_op jit(solution)/shard_map/ppermute | solution.py:338
  220.4 31.7 %collective-permute-start.9 = (bf16[2,256,1024]{2,1,0:T(8,128)(2,1)S(1)}, bf16[2,256,1024]{2,1,0:T(8,128)(2,1)S(1)}, u32[]{:S(2)}, u32[]{:S(2)}) collective-permute-start(bf16[2,256,1024]{2,1,0:T(8,128)(2,1)S(1)} %pad_maximum_fusion.12), channel_id=1, source_target_pairs={{0,2},{2,0},{4,6},{6,4},{8,10},{10,8},{12,14},{14,12},{16,18},{18,... | collective-permute-start | bytes 3145736 | tf_op jit(solution)/shard_map/ppermute | solution.py:338
  222.2 69.6 %collective-permute-start.8 = (bf16[2,256,1024]{2,1,0:T(8,128)(2,1)}, bf16[2,256,1024]{2,1,0:T(8,128)(2,1)}, u32[]{:S(2)}, u32[]{:S(2)}) collective-permute-start(bf16[2,256,1024]{2,1,0:T(8,128)(2,1)} %pad_maximum_fusion.11), channel_id=1, source_target_pairs={{0,2},{2,0},{4,6},{6,4},{8,10},{10,8},{12,14},{14,12},{16,18},{18,... | collective-permute-start | bytes 3145736 | tf_op jit(solution)/shard_map/ppermute | solution.py:338
  227.1 21.3 %collective-permute-start.19 = (bf16[256,1024]{1,0:T(8,128)(2,1)S(1)}, bf16[256,1024]{1,0:T(8,128)(2,1)S(1)}, u32[]{:S(2)}, u32[]{:S(2)}) collective-permute-start(bf16[256,1024]{1,0:T(8,128)(2,1)S(1)} %fusion.105), channel_id=1, source_target_pairs={{0,4},{2,6},{8,0},{10,2},{16,8},{18,10},{24,16},{26,18},{28,24},{3... | collective-permute-start | bytes 1572872 | tf_op jit(solution)/shard_map/ppermute | solution.py:347
  230.4 20.5 %collective-permute-start.12 = (bf16[256,1024]{1,0:T(8,128)(2,1)S(1)}, bf16[256,1024]{1,0:T(8,128)(2,1)S(1)}, u32[]{:S(2)}, u32[]{:S(2)}) collective-permute-start(bf16[256,1024]{1,0:T(8,128)(2,1)S(1)} %fusion.119), channel_id=1, source_target_pairs={{0,8},{2,10},{8,16},{10,18},{16,24},{18,26},{24,28},{26,30},{28,20... | collective-permute-start | bytes 1572872 | tf_op jit(solution)/shard_map/ppermute | solution.py:347
  248.7 18.9 %collective-permute-start.20 = (bf16[256,1024]{1,0:T(8,128)(2,1)S(1)}, bf16[256,1024]{1,0:T(8,128)(2,1)S(1)}, u32[]{:S(2)}, u32[]{:S(2)}) collective-permute-start(bf16[256,1024]{1,0:T(8,128)(2,1)S(1)} %fusion.107), channel_id=1, source_target_pairs={{0,4},{2,6},{8,0},{10,2},{16,8},{18,10},{24,16},{26,18},{28,24},{3... | collective-permute-start | bytes 1572872 | tf_op jit(solution)/shard_map/ppermute | solution.py:347
  251.0 69.3 %collective-permute-start.7 = (bf16[2,256,1024]{2,1,0:T(8,128)(2,1)}, bf16[2,256,1024]{2,1,0:T(8,128)(2,1)}, u32[]{:S(2)}, u32[]{:S(2)}) collective-permute-start(bf16[2,256,1024]{2,1,0:T(8,128)(2,1)} %pad_maximum_fusion.10), channel_id=1, source_target_pairs={{0,2},{2,0},{4,6},{6,4},{8,10},{10,8},{12,14},{14,12},{16,18},{18,... | collective-permute-start | bytes 3145736 | tf_op jit(solution)/shard_map/ppermute | solution.py:338
  252.1 37.5 %collective-permute-start.13 = (bf16[256,1024]{1,0:T(8,128)(2,1)}, bf16[256,1024]{1,0:T(8,128)(2,1)}, u32[]{:S(2)}, u32[]{:S(2)}) collective-permute-start(bf16[256,1024]{1,0:T(8,128)(2,1)} %fusion.121), channel_id=1, source_target_pairs={{0,8},{2,10},{8,16},{10,18},{16,24},{18,26},{24,28},{26,30},{28,20... | collective-permute-start | bytes 1572872 | tf_op jit(solution)/shard_map/ppermute | solution.py:347
  268.8 23.2 %collective-permute-start.21 = (bf16[256,1024]{1,0:T(8,128)(2,1)}, bf16[256,1024]{1,0:T(8,128)(2,1)}, u32[]{:S(2)}, u32[]{:S(2)}) collective-permute-start(bf16[256,1024]{1,0:T(8,128)(2,1)} %fusion.109), channel_id=1, source_target_pairs={{0,4},{2,6},{8,0},{10,2},{16,8},{18,10},{24,16},{26,18},{28,24},{3... | collective-permute-start | bytes 1572872 | tf_op jit(solution)/shard_map/ppermute | solution.py:347
  284.9 68.5 %all-to-all-start.3 = ((bf16[16,2,128,128]{3,2,1,0:T(8,128)(2,1)}), bf16[16,2,128,128]{3,2,1,0:T(8,128)(2,1)}, u32[]{:S(2)}, u32[]{:S(2)}) async-start(bf16[16,2,128,128]{3,2,1,0:T(8,128)(2,1)} %conv_backward.1), calls=%async_computation.3 | async-start | bytes 2097152 | tf_op jit(solution)/shard_map/all_to_all | solution.py:262
  289.6 60.6 %collective-permute-start.6 = (bf16[2,256,1024]{2,1,0:T(8,128)(2,1)}, bf16[2,256,1024]{2,1,0:T(8,128)(2,1)}, u32[]{:S(2)}, u32[]{:S(2)}) collective-permute-start(bf16[2,256,1024]{2,1,0:T(8,128)(2,1)} %pad_maximum_fusion.9), channel_id=1, source_target_pairs={{0,2},{2,0},{4,6},{6,4},{8,10},{10,8},{12,14},{14,12},{16,18},{18,... | collective-permute-start | bytes 3145736 | tf_op jit(solution)/shard_map/ppermute | solution.py:338
  291.8 86.4 %collective-permute-start.5 = (bf16[2,256,1024]{2,1,0:T(8,128)(2,1)}, bf16[2,256,1024]{2,1,0:T(8,128)(2,1)}, u32[]{:S(2)}, u32[]{:S(2)}) collective-permute-start(bf16[2,256,1024]{2,1,0:T(8,128)(2,1)} %pad_maximum_fusion.8), channel_id=1, source_target_pairs={{0,2},{2,0},{4,6},{6,4},{8,10},{10,8},{12,14},{14,12},{16,18},{18,... | collective-permute-start | bytes 3145736 | tf_op jit(solution)/shard_map/ppermute | solution.py:338
  291.9 26.9 %collective-permute-start.14 = (bf16[256,1024]{1,0:T(8,128)(2,1)S(1)}, bf16[256,1024]{1,0:T(8,128)(2,1)S(1)}, u32[]{:S(2)}, u32[]{:S(2)}) collective-permute-start(bf16[256,1024]{1,0:T(8,128)(2,1)S(1)} %fusion.123), channel_id=1, source_target_pairs={{0,8},{2,10},{8,16},{10,18},{16,24},{18,26},{24,28},{26,30},{28,20... | collective-permute-start | bytes 1572872 | tf_op jit(solution)/shard_map/ppermute | solution.py:347
  295.4 32.0 %collective-permute-start.22 = (bf16[256,1024]{1,0:T(8,128)(2,1)S(1)}, bf16[256,1024]{1,0:T(8,128)(2,1)S(1)}, u32[]{:S(2)}, u32[]{:S(2)}) collective-permute-start(bf16[256,1024]{1,0:T(8,128)(2,1)S(1)} %fusion.111), channel_id=1, source_target_pairs={{0,4},{2,6},{8,0},{10,2},{16,8},{18,10},{24,16},{26,18},{28,24},{3... | collective-permute-start | bytes 1572872 | tf_op jit(solution)/shard_map/ppermute | solution.py:347
  318.9 70.4 %collective-permute-start.4 = (bf16[2,256,1024]{2,1,0:T(8,128)(2,1)}, bf16[2,256,1024]{2,1,0:T(8,128)(2,1)}, u32[]{:S(2)}, u32[]{:S(2)}) collective-permute-start(bf16[2,256,1024]{2,1,0:T(8,128)(2,1)} %pad_maximum_fusion.7), channel_id=1, source_target_pairs={{0,2},{2,0},{4,6},{6,4},{8,10},{10,8},{12,14},{14,12},{16,18},{18,... | collective-permute-start | bytes 3145736 | tf_op jit(solution)/shard_map/ppermute | solution.py:338
  320.2 25.2 %collective-permute-start.15 = (bf16[256,1024]{1,0:T(8,128)(2,1)S(1)}, bf16[256,1024]{1,0:T(8,128)(2,1)}, u32[]{:S(2)}, u32[]{:S(2)}) collective-permute-start(bf16[256,1024]{1,0:T(8,128)(2,1)S(1)} %fusion.125), channel_id=1, source_target_pairs={{0,8},{2,10},{8,16},{10,18},{16,24},{18,26},{24,28},{26,30},{28,20... | collective-permute-start | bytes 1572872 | tf_op jit(solution)/shard_map/ppermute | solution.py:347
  329.6 20.6 %collective-permute-start.23 = (bf16[256,1024]{1,0:T(8,128)(2,1)}, bf16[256,1024]{1,0:T(8,128)(2,1)}, u32[]{:S(2)}, u32[]{:S(2)}) collective-permute-start(bf16[256,1024]{1,0:T(8,128)(2,1)} %fusion.113), channel_id=1, source_target_pairs={{0,4},{2,6},{8,0},{10,2},{16,8},{18,10},{24,16},{26,18},{28,24},{3... | collective-permute-start | bytes 1572872 | tf_op jit(solution)/shard_map/ppermute | solution.py:347
  347.7 19.3 %collective-permute-start.16 = (bf16[256,1024]{1,0:T(8,128)(2,1)}, bf16[256,1024]{1,0:T(8,128)(2,1)}, u32[]{:S(2)}, u32[]{:S(2)}) collective-permute-start(bf16[256,1024]{1,0:T(8,128)(2,1)} %fusion.127), channel_id=1, source_target_pairs={{0,8},{2,10},{8,16},{10,18},{16,24},{18,26},{24,28},{26,30},{28,20... | collective-permute-start | bytes 1572872 | tf_op jit(solution)/shard_map/ppermute | solution.py:347
  352.5 25.6 %collective-permute-start.24 = (bf16[256,1024]{1,0:T(8,128)(2,1)}, bf16[256,1024]{1,0:T(8,128)(2,1)}, u32[]{:S(2)}, u32[]{:S(2)}) collective-permute-start(bf16[256,1024]{1,0:T(8,128)(2,1)} %fusion.115), channel_id=1, source_target_pairs={{0,4},{2,6},{8,0},{10,2},{16,8},{18,10},{24,16},{26,18},{28,24},{3... | collective-permute-start | bytes 1572872 | tf_op jit(solution)/shard_map/ppermute | solution.py:347
  365.6 6.4 %collective-permute-start.3 = (bf16[3,2,6,2048]{3,2,1,0:T(8,128)(2,1)S(1)}, bf16[3,2,6,2048]{3,2,1,0:T(8,128)(2,1)S(1)}, u32[]{:S(2)}, u32[]{:S(2)}) collective-permute-start(bf16[3,2,6,2048]{3,2,1,0:T(8,128)(2,1)S(1)} %pad_maximum_fusion.16), channel_id=1, source_target_pairs={{2,0},{4,2},{6,4},{8,6},{10,8},{12,10},{14,12},{16,14},{18,16},{20... | collective-permute-start | bytes 442376 | tf_op jit(solution)/shard_map/ppermute | solution.py:20
  368.6 15.9 %collective-permute-start.17 = (bf16[256,1024]{1,0:T(8,128)(2,1)S(1)}, bf16[256,1024]{1,0:T(8,128)(2,1)S(1)}, u32[]{:S(2)}, u32[]{:S(2)}) collective-permute-start(bf16[256,1024]{1,0:T(8,128)(2,1)S(1)} %fusion.129), channel_id=1, source_target_pairs={{0,8},{2,10},{8,16},{10,18},{16,24},{18,26},{24,28},{26,30},{28,20... | collective-permute-start | bytes 1572872 | tf_op jit(solution)/shard_map/ppermute | solution.py:347
  379.7 14.0 %collective-permute-start.25 = (bf16[256,1024]{1,0:T(8,128)(2,1)S(1)}, bf16[256,1024]{1,0:T(8,128)(2,1)S(1)}, u32[]{:S(2)}, u32[]{:S(2)}) collective-permute-start(bf16[256,1024]{1,0:T(8,128)(2,1)S(1)} %fusion.117), channel_id=1, source_target_pairs={{0,4},{2,6},{8,0},{10,2},{16,8},{18,10},{24,16},{26,18},{28,24},{3... | collective-permute-start | bytes 1572872 | tf_op jit(solution)/shard_map/ppermute | solution.py:347
  385.9 13.4 %collective-permute-start.18 = (bf16[256,1024]{1,0:T(8,128)(2,1)S(1)}, bf16[256,1024]{1,0:T(8,128)(2,1)S(1)}, u32[]{:S(2)}, u32[]{:S(2)}) collective-permute-start(bf16[256,1024]{1,0:T(8,128)(2,1)S(1)} %fusion.131), channel_id=1, source_target_pairs={{0,8},{2,10},{8,16},{10,18},{16,24},{18,26},{24,28},{26,30},{28,20... | collective-permute-start | bytes 1572872 | tf_op jit(solution)/shard_map/ppermute | solution.py:347
  (7 other events, 68.0 us)
Sparse Core Ops, SparseCore 0:
  10.2 171.5 all-gather.1
